TPU v7x, 128 devices: a whole 4x4x4 slice. The times are simulated.
128 devices in a mesh: blk: 8 (over z_hi, x), seg: 16 (over z_lo, y, core).
Axes of the slice: x: 4, y: 4, z: 4 (z_hi: 2, z_lo: 2; z = z_hi * 2 + z_lo), core: 2. Of those that a mesh axis runs over, the one named last changes fastest.
Arguments:
- spectra: bfloat16 [16, 1024, 2, 4096], P(None, ('blk', 'seg')), may hold values from -6 to 6
- fibre_lists: int32 [16, 64], replicated, may hold values from 0 to 1023, as said below
- pairing: int32 [1, 16], replicated, may hold values from 0 to 15, as said below
Outputs:
- stack: float32 [1, 16, 64, 64, 128], P(None, 'blk', 'seg')
Inputs may be any that keep to these rules, and one draw needn't show every extreme that they name: `fibre_lists`: row b lists the 64 channels of block b in an arbitrary order; every channel number appears exactly once in the table. Within every aligned range of 128 consecutive channel numbers, no block has more than 12 of its channels, and some block has exactly 12. `pairing`: row r maps every block to its partner in round r: the partner of the partner is the block itself, no block is its own partner, and no two rounds pair the same two blocks.
All inputs are finite; a program needn't handle non-finite values.
Results may differ from a plain program's by a relative error of at most 0.0037.
Values may be sent and summed in bfloat16 or wider, within the bound.
No kernel may reach another device: no remote copies, remote signals or barrier semaphores. Data moves between devices by JAX's collectives and lax.ppermute only.
A program may use at most 192 MiB of HBM per device.

v0:
```python
import math

import jax
import jax.numpy as jnp
from jax import lax
from jax.sharding import PartitionSpec as P

LH = 128


def make_table(frequencies, lag_count):
    freq_ids = jnp.arange(frequencies, dtype=jnp.int32)[:, None]
    lag_ids = jnp.arange(lag_count, dtype=jnp.int32)[None, :]
    angles = (freq_ids * lag_ids % (2 * frequencies)).astype(jnp.float32) * (math.pi / frequencies)
    return jnp.concatenate([jnp.cos(angles), -jnp.sin(angles)], 0).astype(jnp.bfloat16)


def cross_lags(left_rows, right_rows, lag_table):
    left_re = left_rows[:, 0].astype(jnp.float32)
    left_im = left_rows[:, 1].astype(jnp.float32)
    right_re = right_rows[:, 0].astype(jnp.float32)
    right_im = right_rows[:, 1].astype(jnp.float32)
    real_part = left_re[:, None, :] * right_re[None] + left_im[:, None, :] * right_im[None]
    imag_part = left_im[:, None, :] * right_re[None] - left_re[:, None, :] * right_im[None]
    spectrum = jnp.concatenate([real_part, imag_part], -1).astype(jnp.bfloat16)
    spectrum = spectrum.reshape(-1, spectrum.shape[-1])
    product = jnp.dot(spectrum, lag_table, preferred_element_type=jnp.float32)
    return product.reshape(left_rows.shape[0], right_rows.shape[0], -1)


def pair_terms(own_panels, others, lag_table, row_count):
    seg_local = own_panels.shape[0]
    blk_local = own_panels.shape[1]
    units = others.shape[1]
    channels = others.shape[2]
    lag_count = lag_table.shape[1]
    sub_rows = math.gcd(row_count, max(1, 512 // channels))

    def unit_term(unit_index):
        left_all = lax.dynamic_index_in_dim(own_panels, unit_index % blk_local, 1, keepdims=False)
        right_all = lax.dynamic_index_in_dim(others, unit_index, 1, keepdims=False)

        def accumulate(step, running):
            left_rows = lax.dynamic_index_in_dim(left_all, step, 0, keepdims=False)
            right_rows = lax.dynamic_index_in_dim(right_all, step, 0, keepdims=False)
            pieces = [
                cross_lags(left_rows[offset : offset + sub_rows], right_rows, lag_table)
                for offset in range(0, row_count, sub_rows)
            ]
            return running + jnp.concatenate(pieces, 0)

        return lax.fori_loop(
            0, seg_local, accumulate, jnp.zeros((row_count, channels, lag_count), jnp.float32)
        )

    terms = lax.map(unit_term, jnp.arange(units, dtype=jnp.int32))
    return jnp.moveaxis(terms, 1, 0).reshape(
        row_count, units // blk_local, blk_local, channels, lag_count
    )


def local(spectra, fibre_lists, pairing):
    frequencies = spectra.shape[-1]
    blk_count = lax.axis_size("blk")
    seg_count = lax.axis_size("seg")
    blk_index = lax.axis_index("blk")
    block_count, channels = fibre_lists.shape
    blk_local = block_count // blk_count
    bound_rows = 3 * channels // (2 * blk_count)
    column = lax.all_to_all(spectra, "seg", split_axis=0, concat_axis=1, tiled=True)
    seg_local = column.shape[0]
    width = column.shape[1]
    mine_ids = blk_index * blk_local + jnp.arange(blk_local, dtype=jnp.int32)
    partners = jnp.take(pairing, mine_ids, axis=1).reshape(-1)
    local_rows = fibre_lists - blk_index * width
    inside = (local_rows >= 0) & (local_rows < width)
    outgoing = jnp.sort(jnp.where(inside, local_rows, width), axis=1)[:, :bound_rows]
    packed = jnp.take(column, outgoing.reshape(-1), axis=1, mode="fill", fill_value=0)
    packed = packed.reshape(seg_local, blk_count, blk_local * bound_rows, 2, frequencies)
    arrived = lax.all_to_all(packed, "blk", split_axis=1, concat_axis=1, tiled=True)
    arrived = arrived.reshape(seg_local, blk_count * blk_local * bound_rows, 2, frequencies)
    wanted = jnp.take(fibre_lists, mine_ids, axis=0)
    source = wanted // width
    same_column = (source[:, :, None] == source[:, None, :]) & (
        wanted[:, None, :] < wanted[:, :, None]
    )
    rank_within = jnp.sum(same_column.astype(jnp.int32), axis=2)
    slot_index = (
        source * (blk_local * bound_rows)
        + jnp.arange(blk_local, dtype=jnp.int32)[:, None] * bound_rows
        + rank_within
    )
    own_panels = jnp.take(arrived, slot_index.reshape(-1), axis=1).reshape(
        seg_local, blk_local, channels, 2, frequencies
    )
    panels = lax.all_gather(own_panels, "blk", axis=1, tiled=True)
    others = jnp.take(panels, partners, axis=1)
    lag_table = make_table(frequencies, LH)
    share_rows = channels // seg_count
    scaling = 1.0 / math.sqrt(frequencies * seg_local * seg_count)
    summed = lax.psum(pair_terms(own_panels, others, lag_table, channels), "seg")
    kept_rows = lax.dynamic_slice_in_dim(summed, lax.axis_index("seg") * share_rows, share_rows, 0)
    return jnp.transpose(kept_rows, (1, 2, 0, 3, 4)) * scaling


def solution(mesh):
    in_specs = (P(None, ("blk", "seg"), None, None), P(), P())
    out_specs = P(None, "blk", "seg", None, None)
    return jax.shard_map(local, mesh=mesh, in_specs=in_specs, out_specs=out_specs, check_vma=False)
```

profile of v0, /device:TPU:0, one launch (start us, length us, event | category | flops | bytes accessed | tf_op | source)
XLA Modules:
  0.0 600.3 jit_solution(15975505315950947489)
XLA Ops:
  6.5 6.2 %all-to-all-start = ((bf16[16,8,2,4096]{3,2,1,0:T(2,128)(2,1)}), bf16[16,8,2,4096]{3,2,1,0:T(2,128)(2,1)S(1)}, u32[]{:S(2)}, u32[]{:S(2)}) async-start(bf16[16,8,2,4096]{3,2,1,0:T(2,128)(2,1)} %param.5), calls=%async_computation | async-start | bytes 4194304 | tf_op jit(solution)/shard_map/all_to_all | solution.py:70
  14.1 26.7 %all-to-all-done = bf16[16,8,2,4096]{3,2,1,0:T(2,128)(2,1)S(1)} async-done(((bf16[16,8,2,4096]{3,2,1,0:T(2,128)(2,1)}), bf16[16,8,2,4096]{3,2,1,0:T(2,128)(2,1)S(1)}, u32[]{:S(2)}, u32[]{:S(2)}) %all-to-all-start) | async-done | bytes 2097184 | tf_op jit(solution)/shard_map/all_to_all | solution.py:70
  40.8 11.0 %gather_fusion.1 = bf16[192,2,4096]{2,1,0:T(2,128)(2,1)} fusion(bf16[128,2,4096]{2,1,0:T(2,128)(2,1)S(1)} %bitcast.207, s32[1024]{0:T(1024)S(1)} %pad_clamp_fusion.2), kind=kCustom, calls=%fused_computation.1 | custom fusion | bytes 6292224 | tf_op jit(solution)/shard_map/jit(_take)/gather | solution.py:78
  51.8 6.3 %broadcast_select_fusion = bf16[1,8,24,2,4096]{4,3,2,0,1:T(2,128)(2,1)} fusion(bf16[1,8,24,2,4096]{4,3,2,0,1:T(2,128)(2,1)} %bitcast.208, pred[8,24]{1,0:T(8,128)(4,1)S(1)} %compare_and_fusion), kind=kLoop, calls=%fused_computation.124 | loop fusion | flops 1572864 | bytes 6291648 | tf_op jit(solution)/shard_map/jit(_take)/select_n | solution.py:78
  58.1 7.3 %all-to-all-start.1 = ((bf16[1,8,24,2,4096]{4,3,2,0,1:T(2,128)(2,1)}), bf16[1,8,24,2,4096]{4,3,2,0,1:T(2,128)(2,1)S(1)}, u32[]{:S(2)}, u32[]{:S(2)}) async-start(bf16[1,8,24,2,4096]{4,3,2,0,1:T(2,128)(2,1)} %broadcast_select_fusion), calls=%async_computation.1 | async-start | bytes 6291456 | tf_op jit(solution)/shard_map/all_to_all | solution.py:80
  67.0 38.2 %all-to-all-done.1 = bf16[1,8,24,2,4096]{4,3,2,0,1:T(2,128)(2,1)S(1)} async-done(((bf16[1,8,24,2,4096]{4,3,2,0,1:T(2,128)(2,1)}), bf16[1,8,24,2,4096]{4,3,2,0,1:T(2,128)(2,1)S(1)}, u32[]{:S(2)}, u32[]{:S(2)}) %all-to-all-start.1) | async-done | bytes 3145760 | tf_op jit(solution)/shard_map/all_to_all | solution.py:80
  105.2 8.0 %gather_fusion.2 = bf16[128,2,4096]{2,1,0:T(2,128)(2,1)} fusion(bf16[192,2,4096]{2,1,0:T(2,128)(2,1)S(1)} %bitcast.209, s32[1024]{0:T(1024)S(1)} %pad_clamp_fusion.1), kind=kCustom, calls=%fused_computation.2 | custom fusion | bytes 4194816 | tf_op jit(solution)/shard_map/jit(_take)/gather | solution.py:93
  113.2 2.9 copy.22
  118.5 8.6 %negate_convert_fusion = (bf16[4096,128]{1,0:T(8,128)(2,1)S(1)}, bf16[4096,128]{1,0:T(8,128)(2,1)S(1)}) fusion(), kind=kLoop, calls=%fused_computation.133 | loop fusion | flops 8912896 | bytes 2097152 | tf_op jit(solution)/shard_map/convert.35
  128.5 181.5 %all-gather.2.cloned.1.call-done = bf16[1,16,64,2,4096]{4,2,1,3,0:T(8,128)(2,1)} async-done(((bf16[1,2,64,2,4096]{4,2,1,3,0:T(8,128)(2,1)}), bf16[1,16,64,2,4096]{4,2,1,3,0:T(8,128)(2,1)}) %all-gather.2.cloned.1.call-update) | async-done | bytes 16777232 | tf_op jit(solution)/shard_map/all_gather | solution.py:96
  310.0 7.9 %gather_fusion.4 = bf16[2,64,2,4096]{3,1,2,0:T(8,128)(2,1)} fusion(bf16[16,64,2,4096]{3,1,0,2:T(8,128)(2,1)} %bitcast.211, s32[1024]{0:T(1024)S(1)} %pad_clamp_fusion), kind=kCustom, calls=%fused_computation.4 | custom fusion | bytes 4194312 | tf_op jit(solution)/shard_map/jit(_take)/gather | solution.py:97
  317.9 3.2 bitcast_select_fusion
  321.1 143.0 %while.13 = (s32[]{:T(128)}, f32[2,64,64,128]{3,2,1,0:T(8,128)}, s32[2]{0:T(128)S(1)}, bf16[1,2,64,2,4096]{4,2,1,3,0:T(8,128)(2,1)S(1)}, bf16[1,2,64,2,4096]{4,2...) while((s32[]{:T(128)}, f32[2,64,64,128]{3,2,1,0:T(8,128)}, ...), condition=%wide.region_3.4_spmd, body=%wide.region_2.3_spmd.sunk | while | flops 8859418624 | bytes 385877280 | solution.py:56
  328.3 28.8 %add_convert_fusion.9 = (bf16[8,64,4096]{2,1,0:T(8,128)(2,1)S(1)}, bf16[8,64,4096]{2,1,0:T(8,128)(2,1)S(1)}, bf16[8,64,4096]{2,1,0:T(8,128)(2,1)}, bf16[8,64,409...) fusion(f32[8,4096]{1,0:T(8,128)S(1)} %copy-done.17, ...), kind=kLoop, calls=%fused_computation.38.clone.1 | loop fusion | flops 134217728 | bytes 71303168 | tf_op jit(solution)/shard_map/convert.18
  357.2 5.9 fusion.165
  363.7 4.1 fusion.166
  367.8 4.1 fusion.167
  371.9 4.1 fusion.168
  376.1 4.1 fusion.169
  380.2 4.1 fusion.170
  384.3 4.1 fusion.171
  388.4 2.7 fusion.172
  399.9 28.8 %add_convert_fusion.9 = (bf16[8,64,4096]{2,1,0:T(8,128)(2,1)S(1)}, bf16[8,64,4096]{2,1,0:T(8,128)(2,1)S(1)}, bf16[8,64,4096]{2,1,0:T(8,128)(2,1)}, bf16[8,64,409...) fusion(f32[8,4096]{1,0:T(8,128)S(1)} %copy-done.17, ...), kind=kLoop, calls=%fused_computation.38.clone.1 | loop fusion | flops 134217728 | bytes 71303168 | tf_op jit(solution)/shard_map/convert.18
  428.7 5.9 fusion.165
  435.2 4.1 fusion.166
  439.3 4.1 fusion.167
  443.5 4.1 fusion.168
  447.6 4.1 fusion.169
  451.7 4.1 fusion.170
  455.8 4.1 fusion.171
  459.9 2.7 fusion.172
  464.1 127.6 %all-reduce.2.cloned.1.call-done = f32[64,1,2,64,128]{4,3,0,2,1:T(8,128)} async-done(((f32[64,1,2,64,128]{4,3,0,2,1:T(8,128)}), f32[64,1,2,64,128]{4,3,0,2,1:T(8,128)}) %all-reduce.2.cloned.1.call-update) | async-done | bytes 4194320 | tf_op jit(solution)/shard_map/psum | solution.py:101
  (134 shorter events, 20.5 us)
Async XLA Ops:
  6.5 111.3 %copy-start = (s32[1,16]{1,0:T(1,128)S(1)}, s32[1,16]{1,0:T(1,128)}, u32[]{:S(2)}) copy-start(s32[1,16]{1,0:T(1,128)} %param.7) | copy-start | bytes 196
  6.5 6.2 %copy-start.20 = (s32[16,64]{1,0:T(8,128)S(1)}, s32[16,64]{1,0:T(8,128)}, u32[]{:S(2)}) copy-start(s32[16,64]{1,0:T(8,128)} %param.6) | copy-start | bytes 12292
  6.5 34.3 %all-to-all-start = ((bf16[16,8,2,4096]{3,2,1,0:T(2,128)(2,1)}), bf16[16,8,2,4096]{3,2,1,0:T(2,128)(2,1)S(1)}, u32[]{:S(2)}, u32[]{:S(2)}) async-start(bf16[16,8,2,4096]{3,2,1,0:T(2,128)(2,1)} %param.5), calls=%async_computation | async-start | bytes 4194304 | tf_op jit(solution)/shard_map/all_to_all | solution.py:70
  58.1 47.1 %all-to-all-start.1 = ((bf16[1,8,24,2,4096]{4,3,2,0,1:T(2,128)(2,1)}), bf16[1,8,24,2,4096]{4,3,2,0,1:T(2,128)(2,1)S(1)}, u32[]{:S(2)}, u32[]{:S(2)}) async-start(bf16[1,8,24,2,4096]{4,3,2,0,1:T(2,128)(2,1)} %broadcast_select_fusion), calls=%async_computation.1 | async-start | bytes 6291456 | tf_op jit(solution)/shard_map/all_to_all | solution.py:80
  65.5 244.6 %all-gather.2.cloned.1.call-start = ((), (), s32[]{:S(2)}) async-start(), calls=%async_computation.2 | async-start | bytes 18874368 | tf_op jit(solution)/shard_map/all_gather | solution.py:96
  117.7 474.1 %all-reduce.2.cloned.1.call-start = ((), (), s32[]{:S(2)}) async-start(), calls=%async_computation.3 | async-start | bytes 8388608 | tf_op jit(solution)/shard_map/psum | solution.py:101
  310.0 11.1 %copy-start.14 = (bf16[1,2,64,2,4096]{4,2,1,3,0:T(8,128)(2,1)S(1)}, bf16[1,2,64,2,4096]{4,2,1,3,0:T(8,128)(2,1)}, u32[]{:S(2)}) copy-start(bf16[1,2,64,2,4096]{4,2,1,3,0:T(8,128)(2,1)} %broadcast_select_fusion.1) | copy-start | bytes 6291460
  357.1 5.9 copy-start.12
  357.2 6.5 %copy-start.13 = (bf16[8,64,4096]{2,1,0:T(8,128)(2,1)S(1)}, bf16[8,64,4096]{2,1,0:T(8,128)(2,1)}, u32[]{:S(2)}) copy-start(bf16[8,64,4096]{2,1,0:T(8,128)(2,1)} %get-tuple-element.317) | copy-start | bytes 12582916 | tf_op jit(solution)/shard_map/while
  363.7 4.1 copy-start.11
  367.8 4.1 copy-start.8
  367.8 4.1 copy-start.9
  371.9 4.1 copy-start.6
  371.9 4.1 copy-start.7
  376.1 4.1 copy-start.4
  376.1 4.1 copy-start.5
  380.2 4.1 copy-start.2
  380.2 4.1 copy-start.3
  384.3 4.1 copy-start.19
  428.7 5.9 copy-start.12
  428.7 6.5 %copy-start.13 = (bf16[8,64,4096]{2,1,0:T(8,128)(2,1)S(1)}, bf16[8,64,4096]{2,1,0:T(8,128)(2,1)}, u32[]{:S(2)}) copy-start(bf16[8,64,4096]{2,1,0:T(8,128)(2,1)} %get-tuple-element.317) | copy-start | bytes 12582916 | tf_op jit(solution)/shard_map/while
  435.2 4.1 copy-start.11
  439.3 4.1 copy-start.8
  439.3 4.1 copy-start.9
  443.4 4.1 copy-start.6
  443.4 4.1 copy-start.7
  447.6 4.1 copy-start.4
  447.6 4.1 copy-start.5
  451.7 4.1 copy-start.2
  451.7 4.1 copy-start.3
  455.8 4.1 copy-start.19
  464.1 129.3 %copy-start.1 = (s32[1,16]{1,0:T(1,128)S(1)}, s32[1,16]{1,0:T(1,128)}, u32[]{:S(2)}) copy-start(s32[1,16]{1,0:T(1,128)} %param.7) | copy-start | bytes 196
  (10 other events, 21.2 us)
Sparse Core Ops, SparseCore 0:
  117.8 192.1 all-gather.1
  464.3 127.4 all-reduce.1
where the time goes:
time: 601 us; the launch traced here: 600 us
  waiting for transfers between devices  374 us (62%)
  other arithmetic  85.4 us (14%)
  matrix products  66.2 us (11%)
  local copies, waits for them, and re-layouts  40.3 us (7%)
  starting transfers between devices  13.8 us (2%)
  between operations  13.5 us (2%)
  loops' own time  7.09 us (1%)
    all_gather x1, waiting for transfers between devices, local(): panels = lax.all_gather(own_panels, 'blk', axis=1, tiled=True)  181 us
    psum x1, waiting for transfers between devices, local(): lax.psum(pair_terms(own_panels, others, lag_table, channels), 'seg')  128 us
    dot_general x16, matrix products, cross_lags(): product = jnp.dot(spectrum, lag_table, preferred_element_type=jnp.float32)  66.2 us
    another operation x3, other arithmetic  66.2 us
    all_to_all x1, waiting for transfers between devices, local(): lax.all_to_all(packed, 'blk', split_axis=1, concat_axis=1, tiled=True)  38.2 us
    all_to_all x1, waiting for transfers between devices, local(): lax.all_to_all(spectra, 'seg', split_axis=0, concat_axis=1, tiled=True)  26.7 us
  transfers between devices with their start and end apart: 4, of which 4 were waited for; matrix products, arithmetic and copies ran while one was open for 2% of the time, Pallas kernels for 0%

commit v1 on v0

v1 whole, which is shorter than its diff:
```python
import functools
import math

import jax
import jax.numpy as jnp
from jax import lax
from jax.experimental import pallas as pl
from jax.experimental.pallas import tpu as pltpu
from jax.sharding import PartitionSpec as P

LH = 128
WIDE = 512


def make_tables(frequencies, lag_count):
    freq_ids = jnp.arange(frequencies, dtype=jnp.int32)[:, None]
    lag_ids = jnp.arange(lag_count, dtype=jnp.int32)[None, :]
    angles = (freq_ids * lag_ids % (2 * frequencies)).astype(jnp.float32) * (math.pi / frequencies)
    return jnp.cos(angles).astype(jnp.bfloat16), (-jnp.sin(angles)).astype(jnp.bfloat16)


def look_up(table, ids):
    hits = ids[:, None] == jnp.arange(table.shape[0], dtype=jnp.int32)[None, :]
    return jnp.sum(jnp.where(hits, table[None, :], 0), axis=1)


def choose_blocks(partner, blk_local):
    count = partner.shape[0]
    step = jnp.bitwise_xor(partner, 1)
    lowest = jnp.arange(count, dtype=jnp.int32)
    reach = 1
    while reach < count // blk_local:
        lowest = jnp.minimum(lowest, look_up(lowest, step))
        step = look_up(step, step)
        reach *= 2
    return 1 - jnp.bitwise_and(lowest, 1)


def pack_kernel(slot_ref, rows_ref, out_ref):
    sources, _, share, frequencies = rows_ref.shape
    dests, _, bound, _ = out_ref.shape
    shape = (dests * bound, sources * share)
    select = (lax.broadcasted_iota(jnp.int32, shape, 0) == slot_ref[...]).astype(jnp.bfloat16)

    def chunk(step, carry):
        span = pl.ds(pl.multiple_of(step * WIDE, WIDE), WIDE)
        for part in range(2):
            rows = rows_ref[:, part, :, span].astype(jnp.float32)
            rows = rows.reshape(sources * share, WIDE).astype(jnp.bfloat16)
            packed = jnp.dot(select, rows, preferred_element_type=jnp.float32)
            out_ref[:, part, :, span] = packed.reshape(dests, bound, WIDE).astype(jnp.bfloat16)
        return carry

    lax.fori_loop(0, frequencies // WIDE, chunk, 0)


def pair_kernel(group, wide, index_ref, rows_ref, cos_ref, sin_ref, own_ref, other_ref, x_re, x_im, y_re, y_im, sum_a, sum_b):
    sources, _, bound, frequencies = rows_ref.shape
    channels = x_re.shape[0]
    lags = cos_ref.shape[1]
    shares, _, share, _ = other_ref.shape
    shape = (2 * channels, sources * bound)
    select = (lax.broadcasted_iota(jnp.int32, shape, 1) == index_ref[...]).astype(jnp.bfloat16)

    def gather(step, carry):
        span = pl.ds(pl.multiple_of(step * WIDE, WIDE), WIDE)
        for part, x_out, y_out in ((0, x_re, y_re), (1, x_im, y_im)):
            rows = rows_ref[:, part, :, span].astype(jnp.float32)
            rows = rows.reshape(sources * bound, WIDE).astype(jnp.bfloat16)
            panel = jnp.dot(select, rows, preferred_element_type=jnp.float32)
            x_out[:, span] = panel[:channels]
            y_out[:, span] = panel[channels:].astype(y_out.dtype)
        return carry

    lax.fori_loop(0, frequencies // WIDE, gather, 0)

    def block(block_id, carry):
        sum_a[...] = jnp.zeros_like(sum_a)
        sum_b[...] = jnp.zeros_like(sum_b)

        def chunk(step, inner):
            span = pl.ds(pl.multiple_of(step * wide, wide), wide)
            real, imag = [], []
            right_re = [y_re[j : j + 16, span] for j in range(0, channels, 16)]
            right_im = [y_im[j : j + 16, span] for j in range(0, channels, 16)]
            for i in range(group):
                row = pl.ds(block_id * group + i, 1)
                left_re = jnp.broadcast_to(x_re[row, span], (16, wide)).astype(y_re.dtype)
                left_im = jnp.broadcast_to(x_im[row, span], (16, wide)).astype(y_re.dtype)
                for re, im in zip(right_re, right_im):
                    real.append((left_re * re + left_im * im).astype(jnp.bfloat16))
                    imag.append((left_im * re - left_re * im).astype(jnp.bfloat16))
            sum_a[...] += jnp.dot(jnp.concatenate(real, 0), cos_ref[span, :], preferred_element_type=jnp.float32)
            sum_b[...] += jnp.dot(jnp.concatenate(imag, 0), sin_ref[span, :], preferred_element_type=jnp.float32)
            return inner

        lax.fori_loop(0, frequencies // wide, chunk, 0)
        ahead = sum_a[...] + sum_b[...]
        back = (sum_a[...] - sum_b[...]).reshape(group, shares, share, lags)
        own_ref[pl.ds(block_id * group, group)] = ahead.astype(jnp.bfloat16).reshape(group, channels, lags)
        for i in range(group):
            other_ref[:, block_id * group + i] = back[i].astype(jnp.bfloat16)
        return carry

    lax.fori_loop(0, channels // group, block, 0)


def in_vmem(count):
    return [pl.BlockSpec(memory_space=pltpu.VMEM)] * count


def local(spectra, fibre_lists, pairing):
    frequencies = spectra.shape[-1]
    blk_count = lax.axis_size("blk")
    seg_count = lax.axis_size("seg")
    blk_index = lax.axis_index("blk")
    block_count, channels = fibre_lists.shape
    blk_local = block_count // blk_count
    width = blk_local * channels
    side_rows = 3 * channels // (2 * blk_count)
    bound = 2 * side_rows
    share = channels // seg_count

    planar = jnp.transpose(spectra, (0, 2, 1, 3))
    column = lax.all_to_all(planar, "seg", split_axis=0, concat_axis=0, tiled=True)

    partner = pairing[0]
    blocks = jnp.arange(block_count, dtype=jnp.int32)
    chosen = choose_blocks(partner, blk_local)
    worker = jnp.where(chosen == 1, blocks, partner) // blk_local
    source = fibre_lists // width
    earlier = jnp.arange(channels)[None, :] < jnp.arange(channels)[:, None]
    same = (source[:, :, None] == source[:, None, :]) & earlier[None]
    rank = jnp.sum(same.astype(jnp.int32), axis=2)
    side_slot = (1 - chosen)[:, None] * side_rows + rank
    target = worker[:, None] * bound + side_slot
    numbers = blk_index * width + jnp.arange(width, dtype=jnp.int32)
    found = fibre_lists.reshape(-1)[:, None] == numbers[None, :]
    send_slot = jnp.sum(jnp.where(found, target.reshape(-1)[:, None], 0), axis=0)

    own_first = blk_index * blk_local
    own_block = own_first + jnp.sum(jnp.where(blocks == own_first, 1 - chosen, 0))
    other_block = jnp.sum(jnp.where(blocks == own_block, partner, 0))
    arrived_slot = source * bound + side_slot
    wanted = jnp.stack([own_block, other_block])[:, None] == blocks[None, :]
    index = jnp.sum(jnp.where(wanted[:, :, None], arrived_slot[None], 0), axis=1).reshape(-1, 1)

    packed = pl.pallas_call(
        pack_kernel,
        out_shape=jax.ShapeDtypeStruct((blk_count, 2, bound, frequencies), jnp.bfloat16),
        in_specs=in_vmem(2),
        out_specs=in_vmem(1)[0],
        compiler_params=pltpu.CompilerParams(vmem_limit_bytes=24 * 2**20),
    )(send_slot.reshape(1, width), column)
    arrived = lax.all_to_all(packed, "blk", split_axis=0, concat_axis=0, tiled=True)

    cos_table, sin_table = make_tables(frequencies, LH)
    group, wide = 16, 512
    own_part, other_part = pl.pallas_call(
        functools.partial(pair_kernel, group, wide),
        out_shape=[
            jax.ShapeDtypeStruct((channels, channels, LH), jnp.bfloat16),
            jax.ShapeDtypeStruct((seg_count, channels, share, LH), jnp.bfloat16),
        ],
        in_specs=in_vmem(4),
        out_specs=in_vmem(2),
        scratch_shapes=[pltpu.VMEM((channels, frequencies), jnp.float32)] * 4
        + [pltpu.VMEM((group * channels, LH), jnp.float32)] * 2,
        compiler_params=pltpu.CompilerParams(vmem_limit_bytes=40 * 2**20),
    )(index, arrived, cos_table, sin_table)

    scaling = 1.0 / math.sqrt(frequencies * seg_count)
    other_sums = lax.all_to_all(other_part, "seg", split_axis=0, concat_axis=0, tiled=True)
    other_rows = jnp.sum(other_sums.astype(jnp.float32), axis=0) * scaling
    other_rows = jnp.transpose(other_rows, (1, 0, 2)).astype(jnp.bfloat16)
    own_part = own_part.reshape(seg_count, share, channels, LH)
    own_sums = lax.all_to_all(own_part, "seg", split_axis=0, concat_axis=0, tiled=True)
    own_rows = jnp.sum(own_sums.astype(jnp.float32), axis=0) * scaling

    everyone = jnp.broadcast_to(other_rows[None], (blk_count,) + other_rows.shape)
    offered = lax.all_to_all(everyone, "blk", split_axis=0, concat_axis=0, tiled=True)
    lacking = 2 * own_first + blk_local - 1 - own_block
    giver = jnp.sum(jnp.where(blocks == lacking, worker, 0))
    taken = lax.dynamic_index_in_dim(offered, giver, 0, keepdims=False).astype(jnp.float32)
    own_is_first = own_block == own_first
    first = jnp.where(own_is_first, own_rows, taken)
    second = jnp.where(own_is_first, taken, own_rows)
    return jnp.stack([first, second])[None]


def solution(mesh):
    in_specs = (P(None, ("blk", "seg"), None, None), P(), P())
    out_specs = P(None, "blk", "seg", None, None)
    return jax.shard_map(local, mesh=mesh, in_specs=in_specs, out_specs=out_specs, check_vma=False)
```

time: 601 us -> 187 us (0.31)
  waiting for transfers between devices: 374 us -> 79.2 us
  other arithmetic: 85.4 us -> 14.4 us
  matrix products: 66.2 us -> 0 us
  local copies, waits for them, and re-layouts: 40.3 us -> 9.55 us
  Pallas kernels: 0 us -> 29.4 us
  blocking collectives: 0 us -> 20 us
  starting transfers between devices: 13.8 us -> 30.7 us
  between operations: 13.5 us -> 2.7 us
  loops' own time: 7.09 us -> 0 us
    all_gather x1 -> x0, waiting for transfers between devices: 181 us -> none  [local(): panels = lax.all_gather(own_panels, 'blk', axis=1, tiled=True)]
    psum x1 -> x0, waiting for transfers between devices: 128 us -> none  [local(): lax.psum(pair_terms(own_panels, others, lag_table, channels), 'seg')]
    dot_general x16 -> x0, matrix products: 66.2 us -> none  [cross_lags(): product = jnp.dot(spectrum, lag_table, preferred_element_type=jnp.float32)]
    another operation x3 -> x1, other arithmetic: 66.2 us -> 0.62 us  [local(): wanted = jnp.stack([own_block, other_block])[:, None] == blocks[None, :]]
    gather x6 -> x0, local copies, waits for them, and re-layouts: 31 us -> none  [the longest x1 11 us: local(): jnp.take(column, outgoing.reshape(-1), axis=1, mode='fill', fill_value=0)]
    pallas_call x0 -> x2, Pallas kernels: none -> 29.4 us  [the longest x1 27.3 us: local(): pl.pallas_call(functools.partial(pair_kernel, group, wide), out_shape=[ja...]
    all_to_all x0 -> x1, blocking collectives: none -> 20 us  [local(): lax.all_to_all(other_part, 'seg', split_axis=0, concat_axis=0, tiled=True)]
    all_to_all x2 -> x4, starting transfers between devices: 13.5 us -> 30.7 us  [the longest x1 13.6 us: local(): lax.all_to_all(everyone, 'blk', split_axis=0, concat_axis=0, tiled=True)]
  transfers between devices with their start and end apart: 4 -> 4, of which waited for: 4 -> 4; matrix products, arithmetic and copies ran while one was open for 2% -> 7% of each run, Pallas kernels for 0% -> 0%
where the time goes in v1:
time: 187 us; the launch traced here: 186 us
  waiting for transfers between devices  79.2 us (42%)
  starting transfers between devices  30.7 us (16%)
  Pallas kernels  29.4 us (16%)
  blocking collectives  20 us (11%)
  other arithmetic  14.4 us (8%)
  local copies, waits for them, and re-layouts  9.55 us (5%)
  between operations  2.7 us (1%)
    all_to_all x1, waiting for transfers between devices, local(): lax.all_to_all(packed, 'blk', split_axis=0, concat_axis=0, tiled=True)  29.5 us
    pallas_call x1, Pallas kernels, local(): pl.pallas_call(functools.partial(pair_kernel, group, wide), out_shape=[ja...  27.3 us
    all_to_all x1, waiting for transfers between devices, local(): lax.all_to_all(planar, 'seg', split_axis=0, concat_axis=0, tiled=True)  24.4 us
    all_to_all x1, blocking collectives, local(): lax.all_to_all(other_part, 'seg', split_axis=0, concat_axis=0, tiled=True)  20 us
    all_to_all x1, waiting for transfers between devices, local(): lax.all_to_all(own_part, 'seg', split_axis=0, concat_axis=0, tiled=True)  15.9 us
    all_to_all x1, starting transfers between devices, local(): lax.all_to_all(everyone, 'blk', split_axis=0, concat_axis=0, tiled=True)  13.6 us
    all_to_all x1, waiting for transfers between devices, local(): lax.all_to_all(everyone, 'blk', split_axis=0, concat_axis=0, tiled=True)  9.39 us
    convert_element_type x1, other arithmetic, make_tables(): (-jnp.sin(angles)).astype(jnp.bfloat16)  9.31 us
  transfers between devices with their start and end apart: 4, of which 4 were waited for; matrix products, arithmetic and copies ran while one was open for 7% of the time, Pallas kernels for 0%

profile of v1, /device:TPU:0, one launch (start us, length us, event | category | flops | bytes accessed | tf_op | source)
XLA Modules:
  0.0 185.9 jit_solution(868793127507750170)
XLA Ops:
  0.0 4.2 %copy.13 = bf16[16,8,2,4096]{3,1,2,0:T(8,128)(2,1)} copy(bf16[16,8,2,4096]{3,2,1,0:T(2,128)(2,1)} %param.3) | data formatting | bytes 4194304 | tf_op args[0]
  4.2 6.2 %all-to-all-start = ((bf16[16,2,8,4096]{3,2,1,0:T(8,128)(2,1)}), bf16[16,2,8,4096]{3,2,1,0:T(8,128)(2,1)S(1)}, u32[]{:S(2)}, u32[]{:S(2)}) async-start(bf16[16,2,8,4096]{3,2,1,0:T(8,128)(2,1)} %bitcast.25), calls=%async_computation | async-start | bytes 4194304 | tf_op jit(solution)/shard_map/all_to_all | solution.py:125
  10.5 0.2 select_reduce_fusion.5
  10.6 0.2 select_reduce_fusion.3
  10.8 0.2 select_reduce_fusion.2
  11.0 0.6 fusion.9
  12.4 0.5 convert_reduce_fusion.2
  12.9 0.7 fusion.11
  13.6 0.1 add_add_fusion
  13.8 0.3 select_reduce_fusion
  14.1 24.4 %all-to-all-done.rows_ref = bf16[16,2,8,4096]{3,2,1,0:T(8,128)(2,1)S(1)} async-done(((bf16[16,2,8,4096]{3,2,1,0:T(8,128)(2,1)}), bf16[16,2,8,4096]{3,2,1,0:T(8,128)(2,1)S(1)}, u32[]{:S(2)}, u32[]{:S(2)}) %all-to-all-start) | async-done | bytes 2097184 | tf_op jit(solution)/shard_map/all_to_all | solution.py:125
  38.5 2.0 %shard_map.37 = bf16[8,2,24,4096]{3,2,1,0:T(8,128)(2,1)S(1)} custom-call(s32[1,128]{1,0:T(1,128)S(1)} %bitcast.24, bf16[16,2,8,4096]{3,2,1,0:T(8,128)(2,1)S(1)} %all-to-all-done.rows_ref), custom_call_target="tpu_custom_call" | custom-call | tf_op jit(solution)/shard_map/pallas_call | solution.py:148
  40.6 1.7 copy-done
  42.2 7.3 %all-to-all-start.1 = ((bf16[8,2,24,4096]{3,2,1,0:T(8,128)(2,1)}), bf16[8,2,24,4096]{3,2,1,0:T(8,128)(2,1)S(1)}, u32[]{:S(2)}, u32[]{:S(2)}) async-start(bf16[8,2,24,4096]{3,2,1,0:T(8,128)(2,1)} %copy-done), calls=%async_computation.1 | async-start | bytes 6291456 | tf_op jit(solution)/shard_map/all_to_all | solution.py:155
  49.5 0.6 pad_add_fusion
  50.1 0.1 iota_compare_fusion.4
  50.2 0.1 select_reduce_fusion.1
  50.3 0.1 reshape.155.index_ref
  50.5 9.3 %negate_convert_fusion = (bf16[4096,128]{1,0:T(8,128)(2,1)}, bf16[4096,128]{1,0:T(8,128)(2,1)}) fusion(), kind=kLoop, calls=%fused_computation.9 | loop fusion | flops 8912896 | bytes 2097152 | tf_op jit(solution)/shard_map/convert_element_type | solution.py:19
  59.8 29.5 %all-to-all-done.1.rows_ref = bf16[8,2,24,4096]{3,2,1,0:T(8,128)(2,1)S(1)} async-done(((bf16[8,2,24,4096]{3,2,1,0:T(8,128)(2,1)}), bf16[8,2,24,4096]{3,2,1,0:T(8,128)(2,1)S(1)}, u32[]{:S(2)}, u32[]{:S(2)}) %all-to-all-start.1) | async-done | bytes 3145760 | tf_op jit(solution)/shard_map/all_to_all | solution.py:155
  89.3 1.2 copy-done.1
  90.5 1.2 copy-done.2
  91.8 27.3 %shard_map.38 = (bf16[64,64,128]{2,1,0:T(8,128)(2,1)S(1)}, bf16[16,64,4,128]{3,2,1,0:T(4,128)(2,1)S(1)}) custom-call(s32[128,1]{1,0:T(8,128)S(1)} %reshape.155.index_ref, bf16[8,2,24,4096]{3,2,1,0:T(8,128)(2,1)S(1)} %all-to-all-done.1.rows_ref, bf16[4096,128]{1,0:T(8,128)(2,1)S(1)} %copy-done.2, bf16[4096,128]{1,0:T(8,128)(2,1)S(1)} %copy-done.1), custom_call_target="tpu_custom_call" | custom-call | tf_op jit(solution)/shard_map/pallas_call | solution.py:159
  119.1 20.0 %all_to_all.25 = bf16[16,64,4,128]{3,2,1,0:T(4,128)(2,1)S(1)} all-to-all(bf16[16,64,4,128]{3,2,1,0:T(4,128)(2,1)S(1)} %get-tuple-element.8), channel_id=1, replica_groups=mesh['blk'=8,'seg'=16] {'seg'}, dimensions={0} | all-to-all | bytes 2097152 | tf_op jit(solution)/shard_map/all_to_all | solution.py:173
  139.1 3.7 %all-to-all-start.2 = ((bf16[16,4,64,128]{3,2,1,0:T(8,128)(2,1)}), bf16[16,4,64,128]{3,2,1,0:T(8,128)(2,1)S(1)}, u32[]{:S(2)}, u32[]{:S(2)}) async-start(bf16[16,4,64,128]{3,2,1,0:T(8,128)(2,1)} %bitcast.23), calls=%async_computation.2 | async-start | bytes 2097152 | tf_op jit(solution)/shard_map/all_to_all | solution.py:177
  142.8 0.4 convert_reduce_fusion
  143.2 15.9 %all-to-all-done.2 = bf16[16,4,64,128]{3,2,1,0:T(8,128)(2,1)S(1)} async-done(((bf16[16,4,64,128]{3,2,1,0:T(8,128)(2,1)}), bf16[16,4,64,128]{3,2,1,0:T(8,128)(2,1)S(1)}, u32[]{:S(2)}, u32[]{:S(2)}) %all-to-all-start.2) | async-done | bytes 1048608 | tf_op jit(solution)/shard_map/all_to_all | solution.py:177
  159.2 0.9 broadcast_in_dim.124
  160.1 13.6 %all-to-all-start.4 = ((bf16[8,4,64,128]{3,2,1,0:T(8,128)(2,1)}), bf16[8,4,64,128]{3,2,1,0:T(8,128)(2,1)S(1)}, u32[]{:S(2)}, u32[]{:S(2)}) async-start(bf16[8,4,64,128]{3,2,1,0:T(8,128)(2,1)} %broadcast_in_dim.124), calls=%async_computation.4 | async-start | bytes 1048576 | tf_op jit(solution)/shard_map/all_to_all | solution.py:181
  175.6 0.2 convert_reduce_fusion.1
  175.7 9.4 %all-to-all-done.4 = bf16[8,4,64,128]{3,2,1,0:T(8,128)(2,1)S(1)} async-done(((bf16[8,4,64,128]{3,2,1,0:T(8,128)(2,1)}), bf16[8,4,64,128]{3,2,1,0:T(8,128)(2,1)S(1)}, u32[]{:S(2)}, u32[]{:S(2)}) %all-to-all-start.4) | async-done | bytes 524320 | tf_op jit(solution)/shard_map/all_to_all | solution.py:181
  185.2 0.7 maximum_bitcast_fusion
  (22 shorter events, 0.3 us)
Async XLA Ops:
  4.2 6.2 %copy-start.5 = (s32[1,16]{1,0:T(1,128)S(1)}, s32[1,16]{1,0:T(1,128)}, u32[]{:S(2)}) copy-start(s32[1,16]{1,0:T(1,128)} %param.5) | copy-start | bytes 196
  4.2 8.1 %copy-start.4 = (s32[16,64]{1,0:T(8,128)S(1)}, s32[16,64]{1,0:T(8,128)}, u32[]{:S(2)}) copy-start(s32[16,64]{1,0:T(8,128)} %param.4) | copy-start | bytes 12292
  4.2 34.3 %all-to-all-start = ((bf16[16,2,8,4096]{3,2,1,0:T(8,128)(2,1)}), bf16[16,2,8,4096]{3,2,1,0:T(8,128)(2,1)S(1)}, u32[]{:S(2)}, u32[]{:S(2)}) async-start(bf16[16,2,8,4096]{3,2,1,0:T(8,128)(2,1)} %bitcast.25), calls=%async_computation | async-start | bytes 4194304 | tf_op jit(solution)/shard_map/all_to_all | solution.py:125
  40.5 1.7 copy-start
  42.2 47.1 %all-to-all-start.1 = ((bf16[8,2,24,4096]{3,2,1,0:T(8,128)(2,1)}), bf16[8,2,24,4096]{3,2,1,0:T(8,128)(2,1)S(1)}, u32[]{:S(2)}, u32[]{:S(2)}) async-start(bf16[8,2,24,4096]{3,2,1,0:T(8,128)(2,1)} %copy-done), calls=%async_computation.1 | async-start | bytes 6291456 | tf_op jit(solution)/shard_map/all_to_all | solution.py:155
  89.3 1.2 copy-start.1
  90.5 1.2 copy-start.2
  119.1 20.0 %copy-start.3 = (bf16[64,64,128]{2,1,0:T(8,128)(2,1)}, bf16[64,64,128]{2,1,0:T(8,128)(2,1)S(1)}, u32[]{:S(2)}) copy-start(bf16[64,64,128]{2,1,0:T(8,128)(2,1)S(1)} %get-tuple-element.7) | copy-start | bytes 3145732
  139.1 20.1 %all-to-all-start.2 = ((bf16[16,4,64,128]{3,2,1,0:T(8,128)(2,1)}), bf16[16,4,64,128]{3,2,1,0:T(8,128)(2,1)S(1)}, u32[]{:S(2)}, u32[]{:S(2)}) async-start(bf16[16,4,64,128]{3,2,1,0:T(8,128)(2,1)} %bitcast.23), calls=%async_computation.2 | async-start | bytes 2097152 | tf_op jit(solution)/shard_map/all_to_all | solution.py:177
  160.1 25.1 %all-to-all-start.4 = ((bf16[8,4,64,128]{3,2,1,0:T(8,128)(2,1)}), bf16[8,4,64,128]{3,2,1,0:T(8,128)(2,1)S(1)}, u32[]{:S(2)}, u32[]{:S(2)}) async-start(bf16[8,4,64,128]{3,2,1,0:T(8,128)(2,1)} %broadcast_in_dim.124), calls=%async_computation.4 | async-start | bytes 1048576 | tf_op jit(solution)/shard_map/all_to_all | solution.py:181

commit v2 on v1

v2 whole, which is shorter than its diff:
```python
import functools
import math

import jax
import jax.numpy as jnp
from jax import lax
from jax.experimental import pallas as pl
from jax.experimental.pallas import tpu as pltpu
from jax.sharding import PartitionSpec as P

LH = 128


def make_table(frequencies, first, count, lag_count):
    freq_ids = first + jnp.arange(count, dtype=jnp.int32)[:, None]
    lag_ids = jnp.arange(lag_count, dtype=jnp.int32)[None, :]
    angles = (freq_ids * lag_ids % (2 * frequencies)).astype(jnp.float32) * (math.pi / frequencies)
    return jnp.concatenate([jnp.cos(angles), -jnp.sin(angles)], 1).astype(jnp.bfloat16)


def look_up(table, ids):
    hits = ids[:, None] == jnp.arange(table.shape[0], dtype=jnp.int32)[None, :]
    return jnp.sum(jnp.where(hits, table[None, :], 0), axis=1)


def choose_blocks(partner, blk_local):
    count = partner.shape[0]
    step = jnp.bitwise_xor(partner, 1)
    lowest = jnp.arange(count, dtype=jnp.int32)
    reach = 1
    while reach < count // blk_local:
        lowest = jnp.minimum(lowest, look_up(lowest, step))
        step = look_up(step, step)
        reach *= 2
    return 1 - jnp.bitwise_and(lowest, 1)


def rows_of(ref, *at):
    part = ref[(slice(None),) + at].astype(jnp.float32)
    return part.reshape(part.shape[0] * part.shape[1], part.shape[2]).astype(jnp.bfloat16)


def dot(left, right):
    return jnp.dot(left, right, preferred_element_type=jnp.float32)


def dot_rows(left, right):
    return lax.dot_general(left, right, (((1,), (1,)), ((), ())), preferred_element_type=jnp.float32)


def pack_kernel(slot_ref, rows_ref, out_ref, staged, sent):
    sources, segments, parts, share, _ = rows_ref.shape
    dests, _, _, bound, size = out_ref.shape
    shape = (dests * bound, sources * share)
    select = (lax.broadcasted_iota(jnp.int32, shape, 0) == slot_ref[...]).astype(jnp.bfloat16)

    def copy_out(step):
        return pltpu.make_async_copy(staged.at[step], out_ref.at[:, step], sent.at[step])

    def segment(step, carry):
        for part in range(parts):
            packed = dot(select, rows_of(rows_ref, step, part))
            staged[step, :, part] = packed.reshape(dests, bound, size).astype(jnp.bfloat16)
        copy_out(step).start()
        return carry

    lax.fori_loop(0, segments, segment, 0, unroll=4)
    for step in range(segments):
        copy_out(step).wait()


def pair_kernel(batch, group, index_ref, rows_ref, table_ref, message_ref, series, spectrum):
    sources, segments, parts, bound, band = rows_ref.shape
    terms = parts * segments
    shares, quads, share, lags = message_ref.shape
    channels = quads // 2
    both = 2 * channels
    shape = (both, sources * bound)
    select = (lax.broadcasted_iota(jnp.int32, shape, 1) == index_ref[...]).astype(jnp.bfloat16)

    def unit(rows, columns, shift):
        row = lax.broadcasted_iota(jnp.int32, (rows, columns), 0)
        column = lax.broadcasted_iota(jnp.int32, (rows, columns), 1)
        return (row + shift == column).astype(jnp.bfloat16)

    turn_band = unit(band, band, 0)
    pick_left = unit(channels, both, channels)
    turn_both = unit(both, both, 0)

    def segment(step, carry):
        for part in range(parts):
            panel = dot(select, rows_of(rows_ref, step, part)).astype(jnp.bfloat16)
            series[pl.ds(part * segments + step, band, stride=terms + 8), :] = dot_rows(turn_band, panel)
        return carry

    lax.fori_loop(0, segments, segment, 0, unroll=4)

    low = lax.broadcasted_iota(jnp.int32, (batch * terms, both), 1) < channels
    term_of = lax.broadcasted_iota(jnp.int32, (channels, batch * terms), 1) // terms

    def frequencies(step, carry):
        starts = [pl.multiple_of((step * batch + f) * (terms + 8), 8) for f in range(batch)]
        block = jnp.concatenate([series[pl.ds(start, terms), :] for start in starts], 0)
        left = dot_rows(pick_left, block.astype(jnp.bfloat16))
        lefts = [jnp.where(term_of == f, left, 0.0).astype(jnp.bfloat16) for f in range(batch)]
        turned = []
        for f in range(batch):
            turned += [-block[f * terms + segments : (f + 1) * terms], block[f * terms : f * terms + segments]]
        turned = pltpu.roll(jnp.concatenate(turned, 0), channels, axis=1)
        right = jnp.where(low, block, turned).astype(jnp.bfloat16)
        crossed = dot(jnp.concatenate(lefts, 0), right)
        for f in range(batch):
            where = pl.ds(pl.multiple_of((step * batch + f) * (channels + 8), 8), channels)
            spectrum[where, :] = crossed[f * channels : (f + 1) * channels]
        return carry

    lax.fori_loop(0, band // batch, frequencies, 0, unroll=8)
    strips = channels // share
    kept = channels // shares

    def lag_rows(step, carry):
        lines = []
        for i in range(group):
            line = spectrum[pl.ds(step * group + i, band, stride=channels + 8), :]
            lines.append(dot_rows(turn_both, line.astype(jnp.bfloat16)).astype(jnp.bfloat16))
        sums = dot(jnp.concatenate(lines, 0), table_ref[...])
        for i in range(group):
            real = sums[i * both : i * both + channels, :lags]
            imag = sums[i * both + channels : (i + 1) * both, lags:]
            ahead = (real + imag).reshape(strips, share, lags).astype(jnp.bfloat16)
            back = (real - imag).reshape(shares, share, lags).astype(jnp.bfloat16)
            row = step * group + i
            message_ref[row // kept, pl.ds((row % kept) * strips, strips)] = ahead
            message_ref[:, channels + row] = back
        return carry

    lax.fori_loop(0, channels // group, lag_rows, 0)


def in_vmem(count):
    return [pl.BlockSpec(memory_space=pltpu.VMEM)] * count


def local(spectra, fibre_lists, pairing):
    frequencies = spectra.shape[-1]
    blk_count = lax.axis_size("blk")
    seg_count = lax.axis_size("seg")
    blk_index = lax.axis_index("blk")
    block_count, channels = fibre_lists.shape
    blk_local = block_count // blk_count
    width = blk_local * channels
    side_rows = 3 * channels // (2 * blk_count)
    bound = 2 * side_rows
    share = channels // seg_count
    segments, holders, parts, _ = spectra.shape
    band = frequencies // seg_count
    bands = spectra.reshape(segments, holders, parts, seg_count, band)
    bands = jnp.transpose(bands, (3, 0, 2, 1, 4))
    column = lax.all_to_all(bands, "seg", split_axis=0, concat_axis=0, tiled=True)

    partner = pairing[0]
    blocks = jnp.arange(block_count, dtype=jnp.int32)
    chosen = choose_blocks(partner, blk_local)
    worker = jnp.where(chosen == 1, blocks, partner) // blk_local
    source = fibre_lists // width
    earlier = jnp.arange(channels)[None, :] < jnp.arange(channels)[:, None]
    same = (source[:, :, None] == source[:, None, :]) & earlier[None]
    rank = jnp.sum(same.astype(jnp.int32), axis=2)
    side_slot = (1 - chosen)[:, None] * side_rows + rank
    target = worker[:, None] * bound + side_slot
    numbers = blk_index * width + jnp.arange(width, dtype=jnp.int32)
    found = fibre_lists.reshape(-1)[:, None] == numbers[None, :]
    send_slot = jnp.sum(jnp.where(found, target.reshape(-1)[:, None], 0), axis=0).reshape(1, width)

    own_first = blk_index * blk_local
    own_block = own_first + jnp.sum(jnp.where(blocks == own_first, 1 - chosen, 0))
    other_block = jnp.sum(jnp.where(blocks == own_block, partner, 0))
    arrived_slot = source * bound + side_slot
    wanted = jnp.stack([other_block, own_block])[:, None] == blocks[None, :]
    index = jnp.sum(jnp.where(wanted[:, :, None], arrived_slot[None], 0), axis=1)
    index = index.reshape(2 * channels, 1)

    packed = pl.pallas_call(
        pack_kernel,
        out_shape=pltpu.HBM((blk_count, segments, parts, bound, band), jnp.bfloat16),
        in_specs=in_vmem(2),
        out_specs=pl.BlockSpec(memory_space=pltpu.HBM),
        scratch_shapes=[
            pltpu.VMEM((segments, blk_count, parts, bound, band), jnp.bfloat16),
            pltpu.SemaphoreType.DMA((segments,)),
        ],
        compiler_params=pltpu.CompilerParams(vmem_limit_bytes=16 * 2**20),
    )(send_slot, column)
    arrived = lax.all_to_all(packed, "blk", split_axis=0, concat_axis=0, tiled=True)

    table = make_table(frequencies, lax.axis_index("seg") * band, band, LH)
    message = pl.pallas_call(
        functools.partial(pair_kernel, 8, 16),
        out_shape=jax.ShapeDtypeStruct((seg_count, 2 * channels, share, LH), jnp.bfloat16),
        in_specs=in_vmem(3),
        out_specs=in_vmem(1)[0],
        scratch_shapes=[
            pltpu.VMEM((band * (parts * segments + 8), 2 * channels), jnp.float32),
            pltpu.VMEM((band * (channels + 8), 2 * channels), jnp.float32),
        ],
        compiler_params=pltpu.CompilerParams(vmem_limit_bytes=40 * 2**20),
    )(index, arrived, table)

    scaling = 1.0 / math.sqrt(frequencies * segments)
    received = lax.all_to_all(message, "seg", split_axis=0, concat_axis=0, tiled=True)
    total = jnp.sum(received.astype(jnp.float32), axis=0) * scaling
    own = total[:channels].reshape(share, channels, LH)
    other = jnp.transpose(total[channels:], (1, 0, 2)).astype(jnp.bfloat16)
    everyone = jnp.broadcast_to(other[None], (blk_count,) + other.shape)
    offered = lax.all_to_all(everyone, "blk", split_axis=0, concat_axis=0, tiled=True)

    lacking = 2 * own_first + blk_local - 1 - own_block
    giver = jnp.sum(jnp.where(blocks == lacking, worker, 0))
    taken = lax.dynamic_index_in_dim(offered, giver, 0, keepdims=False).astype(jnp.float32)
    own_is_first = own_block == own_first
    first = jnp.where(own_is_first, own, taken)
    second = jnp.where(own_is_first, taken, own)
    return jnp.stack([first, second])[None]


def solution(mesh):
    in_specs = (P(None, ("blk", "seg"), None, None), P(), P())
    out_specs = P(None, "blk", "seg", None, None)
    return jax.shard_map(local, mesh=mesh, in_specs=in_specs, out_specs=out_specs, check_vma=False)
```

time: 187 us -> 161 us (0.86)
  Pallas kernels: 29.4 us -> 15.5 us
  blocking collectives: 20 us -> 31.2 us
  other arithmetic: 14.4 us -> 6.03 us
  waiting for transfers between devices: 79.2 us -> 71.7 us
  starting transfers between devices: 30.7 us -> 27.1 us
  local copies, waits for them, and re-layouts: 9.55 us -> 6.91 us
    all_to_all x2 -> x1, waiting for transfers between devices: 40.3 us -> 24.4 us  [local(): lax.all_to_all(bands, 'seg', split_axis=0, concat_axis=0, tiled=True)]
    pallas_call x2, Pallas kernels: 29.4 us -> 15.5 us  [the longest x1 13.2 us: local(): pl.pallas_call(functools.partial(pair_kernel, 8, 16), out_shape=jax.Shape...]
    all_to_all x1, blocking collectives: 20 us -> 31.2 us  [local(): lax.all_to_all(message, 'seg', split_axis=0, concat_axis=0, tiled=True)]
    convert_element_type x2 -> x0, other arithmetic: 9.35 us -> none  [the longest x1 9.31 us: make_tables(): (-jnp.sin(angles)).astype(jnp.bfloat16)]
    all_to_all x1, waiting for transfers between devices: 29.5 us -> 38.1 us  [local(): lax.all_to_all(packed, 'blk', split_axis=0, concat_axis=0, tiled=True)]
    unnamed x13 -> x4, local copies, waits for them, and re-layouts: 8.36 us -> 0.01 us
    reshape x1 -> x3, local copies, waits for them, and re-layouts: 0.14 us -> 5.81 us  [the longest x2 5.67 us: local(): bands = spectra.reshape(segments, holders, parts, seg_count, band)]
    all_to_all x2 -> x1, starting transfers between devices: 9.83 us -> 6.17 us  [local(): lax.all_to_all(bands, 'seg', split_axis=0, concat_axis=0, tiled=True)]
  transfers between devices with their start and end apart: 4 -> 3, of which waited for: 4 -> 3; matrix products, arithmetic and copies ran while one was open for 7% -> 3% of each run, Pallas kernels for 0% -> 0%
where the time goes in v2:
time: 161 us
  waiting for transfers between devices  71.7 us (45%)
  blocking collectives  31.2 us (19%)
  starting transfers between devices  27.1 us (17%)
  Pallas kernels  15.5 us (10%)
  local copies, waits for them, and re-layouts  6.91 us (4%)
  other arithmetic  6.03 us (4%)
  between operations  2.46 us (2%)
    all_to_all x1, waiting for transfers between devices, local(): lax.all_to_all(packed, 'blk', split_axis=0, concat_axis=0, tiled=True)  38.1 us
    all_to_all x1, blocking collectives, local(): lax.all_to_all(message, 'seg', split_axis=0, concat_axis=0, tiled=True)  31.2 us
    all_to_all x1, waiting for transfers between devices, local(): lax.all_to_all(bands, 'seg', split_axis=0, concat_axis=0, tiled=True)  24.4 us
    all_to_all x1, starting transfers between devices, local(): lax.all_to_all(everyone, 'blk', split_axis=0, concat_axis=0, tiled=True)  13.5 us
    pallas_call x1, Pallas kernels, local(): pl.pallas_call(functools.partial(pair_kernel, 8, 16), out_shape=jax.Shape...  13.2 us
    all_to_all x1, waiting for transfers between devices, local(): lax.all_to_all(everyone, 'blk', split_axis=0, concat_axis=0, tiled=True)  9.17 us
    all_to_all x1, starting transfers between devices, local(): lax.all_to_all(packed, 'blk', split_axis=0, concat_axis=0, tiled=True)  7.34 us
    all_to_all x1, starting transfers between devices, local(): lax.all_to_all(bands, 'seg', split_axis=0, concat_axis=0, tiled=True)  6.17 us
  transfers between devices with their start and end apart: 3, of which 3 were waited for; matrix products, arithmetic and copies ran while one was open for 3% of the time, Pallas kernels for 0%

profile of v2, /device:TPU:0, one launch (start us, length us, event | category | flops | bytes accessed | tf_op | source)
XLA Modules:
  0.0 160.9 jit_solution(2122988864948550785)
XLA Ops:
  0.0 3.1 %reshape.157 = bf16[16,8,2,16,256]{4,3,2,1,0:T(8,128)(2,1)S(1)} reshape(bf16[16,8,2,4096]{3,2,1,0:T(2,128)(2,1)} %param.3) | data formatting | bytes 4194304 | tf_op jit(solution)/shard_map/reshape | solution.py:157
  3.2 2.5 %copy.17 = bf16[16,8,2,16,256]{4,1,2,0,3:T(8,128)(2,1)} copy(bf16[16,8,2,16,256]{4,3,2,1,0:T(8,128)(2,1)S(1)} %reshape.157) | data formatting | bytes 4194304 | tf_op jit(solution)/shard_map/reshape | solution.py:157
  5.7 6.2 %all-to-all-start = ((bf16[16,16,2,8,256]{4,3,2,1,0:T(8,128)(2,1)}), bf16[16,16,2,8,256]{4,3,2,1,0:T(8,128)(2,1)S(1)}, u32[]{:S(2)}, u32[]{:S(2)}) async-start(bf16[16,16,2,8,256]{4,3,2,1,0:T(8,128)(2,1)} %bitcast.21), calls=%async_computation | async-start | bytes 4194304 | tf_op jit(solution)/shard_map/all_to_all | solution.py:159
  11.9 0.0 copy-done.1
  11.9 0.2 select_reduce_fusion.5
  12.1 0.2 select_reduce_fusion.3
  12.3 0.2 select_reduce_fusion.2
  12.5 0.6 fusion.9
  13.8 0.0 copy-done
  13.8 0.1 eq.151
  13.9 0.5 convert_reduce_fusion.1
  14.4 0.7 fusion.11
  15.1 0.1 add_add_fusion
  15.1 0.1 add.83
  15.2 0.3 select_reduce_fusion
  15.6 24.4 %all-to-all-done.rows_ref = bf16[16,16,2,8,256]{4,3,2,1,0:T(8,128)(2,1)S(1)} async-done(((bf16[16,16,2,8,256]{4,3,2,1,0:T(8,128)(2,1)}), bf16[16,16,2,8,256]{4,3,2,1,0:T(8,128)(2,1)S(1)}, u32[]{:S(2)}, u32[]{:S(2)}) %all-to-all-start) | async-done | bytes 2097184 | tf_op jit(solution)/shard_map/all_to_all | solution.py:159
  40.0 2.3 %shard_map.37 = bf16[8,16,2,24,256]{4,3,2,1,0:T(8,128)(2,1)} custom-call(s32[1,128]{1,0:T(1,128)S(1)} %bitcast.20, bf16[16,16,2,8,256]{4,3,2,1,0:T(8,128)(2,1)S(1)} %all-to-all-done.rows_ref), custom_call_target="tpu_custom_call" | custom-call | tf_op jit(solution)/shard_map/pallas_call | solution.py:183
  42.3 7.3 %all-to-all-start.1 = ((bf16[8,16,2,24,256]{4,3,2,1,0:T(8,128)(2,1)}), bf16[8,16,2,24,256]{4,3,2,1,0:T(8,128)(2,1)S(1)}, u32[]{:S(2)}, u32[]{:S(2)}) async-start(bf16[8,16,2,24,256]{4,3,2,1,0:T(8,128)(2,1)} %shard_map.37), calls=%async_computation.1 | async-start | bytes 6291456 | tf_op jit(solution)/shard_map/all_to_all | solution.py:194
  49.6 0.7 pad_add_fusion
  50.3 0.1 iota_compare_fusion.4
  50.4 0.1 select_reduce_fusion.1
  50.5 0.1 reshape.156.index_ref
  50.6 0.6 cosine_convert_fusion
  51.3 38.1 %all-to-all-done.1.rows_ref = bf16[8,16,2,24,256]{4,3,2,1,0:T(8,128)(2,1)S(1)} async-done(((bf16[8,16,2,24,256]{4,3,2,1,0:T(8,128)(2,1)}), bf16[8,16,2,24,256]{4,3,2,1,0:T(8,128)(2,1)S(1)}, u32[]{:S(2)}, u32[]{:S(2)}) %all-to-all-start.1) | async-done | bytes 3145760 | tf_op jit(solution)/shard_map/all_to_all | solution.py:194
  89.4 13.2 %shard_map.38 = bf16[16,128,4,128]{3,2,1,0:T(4,128)(2,1)S(1)} custom-call(s32[128,1]{1,0:T(8,128)S(1)} %reshape.156.index_ref, bf16[8,16,2,24,256]{4,3,2,1,0:T(8,128)(2,1)S(1)} %all-to-all-done.1.rows_ref, bf16[256,256]{1,0:T(8,128)(2,1)S(1)} %pad_maximum_fusion.table_ref), custom_call_target="tpu_custom_call" | custom-call | tf_op jit(solution)/shard_map/pallas_call | solution.py:197
  102.6 31.2 %all_to_all.20 = bf16[16,128,4,128]{3,2,1,0:T(4,128)(2,1)S(1)} all-to-all(bf16[16,128,4,128]{3,2,1,0:T(4,128)(2,1)S(1)} %shard_map.38), channel_id=1, replica_groups=mesh['blk'=8,'seg'=16] {'seg'}, dimensions={0} | all-to-all | bytes 4194304 | tf_op jit(solution)/shard_map/all_to_all | solution.py:210
  133.8 0.9 convert_reduce_fusion
  134.7 0.1 broadcast_multiply_fusion
  134.8 0.9 broadcast_in_dim.124
  135.8 13.5 %all-to-all-start.3 = ((bf16[8,4,64,128]{3,2,1,0:T(8,128)(2,1)}), bf16[8,4,64,128]{3,2,1,0:T(8,128)(2,1)S(1)}, u32[]{:S(2)}, u32[]{:S(2)}) async-start(bf16[8,4,64,128]{3,2,1,0:T(8,128)(2,1)} %broadcast_in_dim.124), calls=%async_computation.3 | async-start | bytes 1048576 | tf_op jit(solution)/shard_map/all_to_all | solution.py:215
  151.0 9.2 %all-to-all-done.3 = bf16[8,4,64,128]{3,2,1,0:T(8,128)(2,1)S(1)} async-done(((bf16[8,4,64,128]{3,2,1,0:T(8,128)(2,1)}), bf16[8,4,64,128]{3,2,1,0:T(8,128)(2,1)S(1)}, u32[]{:S(2)}, u32[]{:S(2)}) %all-to-all-start.3) | async-done | bytes 524320 | tf_op jit(solution)/shard_map/all_to_all | solution.py:215
  160.2 0.7 maximum_bitcast_fusion
  (16 shorter events, 0.1 us)
Async XLA Ops:
  5.7 6.2 %copy-start.1 = (s32[1,16]{1,0:T(1,128)S(1)}, s32[1,16]{1,0:T(1,128)}, u32[]{:S(2)}) copy-start(s32[1,16]{1,0:T(1,128)} %param.5) | copy-start | bytes 196
  5.7 8.1 %copy-start = (s32[16,64]{1,0:T(8,128)S(1)}, s32[16,64]{1,0:T(8,128)}, u32[]{:S(2)}) copy-start(s32[16,64]{1,0:T(8,128)} %param.4) | copy-start | bytes 12292
  5.7 34.3 %all-to-all-start = ((bf16[16,16,2,8,256]{4,3,2,1,0:T(8,128)(2,1)}), bf16[16,16,2,8,256]{4,3,2,1,0:T(8,128)(2,1)S(1)}, u32[]{:S(2)}, u32[]{:S(2)}) async-start(bf16[16,16,2,8,256]{4,3,2,1,0:T(8,128)(2,1)} %bitcast.21), calls=%async_computation | async-start | bytes 4194304 | tf_op jit(solution)/shard_map/all_to_all | solution.py:159
  42.3 47.1 %all-to-all-start.1 = ((bf16[8,16,2,24,256]{4,3,2,1,0:T(8,128)(2,1)}), bf16[8,16,2,24,256]{4,3,2,1,0:T(8,128)(2,1)S(1)}, u32[]{:S(2)}, u32[]{:S(2)}) async-start(bf16[8,16,2,24,256]{4,3,2,1,0:T(8,128)(2,1)} %shard_map.37), calls=%async_computation.1 | async-start | bytes 6291456 | tf_op jit(solution)/shard_map/all_to_all | solution.py:194
  135.8 24.4 %all-to-all-start.3 = ((bf16[8,4,64,128]{3,2,1,0:T(8,128)(2,1)}), bf16[8,4,64,128]{3,2,1,0:T(8,128)(2,1)S(1)}, u32[]{:S(2)}, u32[]{:S(2)}) async-start(bf16[8,4,64,128]{3,2,1,0:T(8,128)(2,1)} %broadcast_in_dim.124), calls=%async_computation.3 | async-start | bytes 1048576 | tf_op jit(solution)/shard_map/all_to_all | solution.py:215

commit v3 on v2

--- a/solution.py
+++ b/solution.py
@@ -8,7 +8,10 @@
 from jax.experimental.pallas import tpu as pltpu
 from jax.sharding import PartitionSpec as P
 
+
 LH = 128
+SHARES = (6, 10)
+TURNS = (5, 7, 4, 6, 2, 3, 1)
 
 
 def make_table(frequencies, first, count, lag_count):
@@ -21,6 +24,10 @@
 def look_up(table, ids):
     hits = ids[:, None] == jnp.arange(table.shape[0], dtype=jnp.int32)[None, :]
     return jnp.sum(jnp.where(hits, table[None, :], 0), axis=1)
+
+
+def turn_of(to, start, ring):
+    return (to // ring - start // ring) % 2 * ring + (to - start) % ring
 
 
 def choose_blocks(partner, blk_local):
@@ -35,9 +42,9 @@
     return 1 - jnp.bitwise_and(lowest, 1)
 
 
-def rows_of(ref, *at):
-    part = ref[(slice(None),) + at].astype(jnp.float32)
-    return part.reshape(part.shape[0] * part.shape[1], part.shape[2]).astype(jnp.bfloat16)
+def stacked(parts):
+    rows = jnp.concatenate([part.astype(jnp.float32) for part in parts], 0)
+    return rows.astype(jnp.bfloat16)
 
 
 def dot(left, right):
@@ -48,29 +55,29 @@
     return lax.dot_general(left, right, (((1,), (1,)), ((), ())), preferred_element_type=jnp.float32)
 
 
-def pack_kernel(slot_ref, rows_ref, out_ref, staged, sent):
+def pack_kernel(slot_ref, rows_ref, *out_refs):
     sources, segments, parts, share, _ = rows_ref.shape
-    dests, _, _, bound, size = out_ref.shape
-    shape = (dests * bound, sources * share)
+    bound = out_refs[0].shape[2]
+    shape = (len(out_refs) * bound, sources * share)
     select = (lax.broadcasted_iota(jnp.int32, shape, 0) == slot_ref[...]).astype(jnp.bfloat16)
-
-    def copy_out(step):
-        return pltpu.make_async_copy(staged.at[step], out_ref.at[:, step], sent.at[step])
 
     def segment(step, carry):
         for part in range(parts):
-            packed = dot(select, rows_of(rows_ref, step, part))
-            staged[step, :, part] = packed.reshape(dests, bound, size).astype(jnp.bfloat16)
-        copy_out(step).start()
+            rows = stacked([rows_ref[source, step, part] for source in range(sources)])
+            packed = dot(select, rows).astype(jnp.bfloat16)
+            for turn, out_ref in enumerate(out_refs):
+                out_ref[step, part] = packed[turn * bound : (turn + 1) * bound]
         return carry
 
-    lax.fori_loop(0, segments, segment, 0, unroll=4)
-    for step in range(segments):
-        copy_out(step).wait()
-
-
-def pair_kernel(batch, group, index_ref, rows_ref, table_ref, message_ref, series, spectrum):
-    sources, segments, parts, bound, band = rows_ref.shape
+    lax.fori_loop(0, segments, segment, 0, unroll=segments // 2)
+
+
+def pair_kernel(batch, group, index_ref, table_ref, *refs):
+    rows_refs, (message_ref, series, spectrum) = refs[:-3], refs[-3:]
+    _, parts, bound, band = rows_refs[0].shape
+    sources = len(rows_refs) // len(SHARES)
+    groups = [rows_refs[first : first + sources] for first in range(0, len(rows_refs), sources)]
+    segments = sum(held[0].shape[0] for held in groups)
     terms = parts * segments
     shares, quads, share, lags = message_ref.shape
     channels = quads // 2
@@ -87,13 +94,19 @@
     pick_left = unit(channels, both, channels)
     turn_both = unit(both, both, 0)
 
-    def segment(step, carry):
-        for part in range(parts):
-            panel = dot(select, rows_of(rows_ref, step, part)).astype(jnp.bfloat16)
-            series[pl.ds(part * segments + step, band, stride=terms + 8), :] = dot_rows(turn_band, panel)
-        return carry
-
-    lax.fori_loop(0, segments, segment, 0, unroll=4)
+    before = 0
+    for held in groups:
+
+        def segment(step, carry, before=before, held=held):
+            for part in range(parts):
+                panel = dot(select, stacked([ref[step, part] for ref in held])).astype(jnp.bfloat16)
+                first = part * segments + before + step
+                series[pl.ds(first, band, stride=terms + 8), :] = dot_rows(turn_band, panel)
+            return carry
+
+        each = held[0].shape[0]
+        lax.fori_loop(0, each, segment, 0, unroll=each // 2)
+        before += each
 
     low = lax.broadcasted_iota(jnp.int32, (batch * terms, both), 1) < channels
     term_of = lax.broadcasted_iota(jnp.int32, (channels, batch * terms), 1) // terms
@@ -141,7 +154,7 @@
     return [pl.BlockSpec(memory_space=pltpu.VMEM)] * count
 
 
-def local(spectra, fibre_lists, pairing):
+def stacks(spectra, fibre_lists, pairing):
     frequencies = spectra.shape[-1]
     blk_count = lax.axis_size("blk")
     seg_count = lax.axis_size("seg")
@@ -149,14 +162,19 @@
     block_count, channels = fibre_lists.shape
     blk_local = block_count // blk_count
     width = blk_local * channels
+    ring = blk_count // 2
     side_rows = 3 * channels // (2 * blk_count)
     bound = 2 * side_rows
     share = channels // seg_count
     segments, holders, parts, _ = spectra.shape
     band = frequencies // seg_count
-    bands = spectra.reshape(segments, holders, parts, seg_count, band)
-    bands = jnp.transpose(bands, (3, 0, 2, 1, 4))
-    column = lax.all_to_all(bands, "seg", split_axis=0, concat_axis=0, tiled=True)
+    sizes = [segments * part // sum(SHARES) for part in SHARES]
+    columns, first = [], 0
+    for size in sizes:
+        bands = spectra[first : first + size].reshape(size, holders, parts, seg_count, band)
+        bands = jnp.transpose(bands, (3, 0, 2, 1, 4))
+        columns.append(lax.all_to_all(bands, "seg", split_axis=0, concat_axis=0, tiled=True))
+        first += size
 
     partner = pairing[0]
     blocks = jnp.arange(block_count, dtype=jnp.int32)
@@ -167,7 +185,7 @@
     same = (source[:, :, None] == source[:, None, :]) & earlier[None]
     rank = jnp.sum(same.astype(jnp.int32), axis=2)
     side_slot = (1 - chosen)[:, None] * side_rows + rank
-    target = worker[:, None] * bound + side_slot
+    target = turn_of(worker, blk_index, ring)[:, None] * bound + side_slot
     numbers = blk_index * width + jnp.arange(width, dtype=jnp.int32)
     found = fibre_lists.reshape(-1)[:, None] == numbers[None, :]
     send_slot = jnp.sum(jnp.where(found, target.reshape(-1)[:, None], 0), axis=0).reshape(1, width)
@@ -175,36 +193,43 @@
     own_first = blk_index * blk_local
     own_block = own_first + jnp.sum(jnp.where(blocks == own_first, 1 - chosen, 0))
     other_block = jnp.sum(jnp.where(blocks == own_block, partner, 0))
-    arrived_slot = source * bound + side_slot
+    arrived_slot = turn_of(blk_index, source, ring) * bound + side_slot
     wanted = jnp.stack([other_block, own_block])[:, None] == blocks[None, :]
     index = jnp.sum(jnp.where(wanted[:, :, None], arrived_slot[None], 0), axis=1)
     index = index.reshape(2 * channels, 1)
 
-    packed = pl.pallas_call(
-        pack_kernel,
-        out_shape=pltpu.HBM((blk_count, segments, parts, bound, band), jnp.bfloat16),
-        in_specs=in_vmem(2),
-        out_specs=pl.BlockSpec(memory_space=pltpu.HBM),
-        scratch_shapes=[
-            pltpu.VMEM((segments, blk_count, parts, bound, band), jnp.bfloat16),
-            pltpu.SemaphoreType.DMA((segments,)),
-        ],
-        compiler_params=pltpu.CompilerParams(vmem_limit_bytes=16 * 2**20),
-    )(send_slot, column)
-    arrived = lax.all_to_all(packed, "blk", split_axis=0, concat_axis=0, tiled=True)
+    arrived = []
+    turned = []
+    for turn in range(blk_count):
+        moves = [(k // ring + turn // ring) % 2 * ring + (k + turn) % ring for k in range(blk_count)]
+        turned.append(list(enumerate(moves)))
+    for size, column in zip(sizes, columns):
+        piece = jax.ShapeDtypeStruct((size, parts, bound, band), jnp.bfloat16)
+        pack = pl.pallas_call(
+            pack_kernel,
+            out_shape=[piece] * blk_count,
+            in_specs=in_vmem(2),
+            out_specs=in_vmem(blk_count),
+            compiler_params=pltpu.CompilerParams(vmem_limit_bytes=16 * 2**20),
+        )
+        packed = pack(send_slot, column)
+        pieces = list(packed)
+        for turn in TURNS:
+            pieces[turn] = lax.ppermute(packed[turn], "blk", turned[turn])
+        arrived += pieces
 
     table = make_table(frequencies, lax.axis_index("seg") * band, band, LH)
     message = pl.pallas_call(
         functools.partial(pair_kernel, 8, 16),
         out_shape=jax.ShapeDtypeStruct((seg_count, 2 * channels, share, LH), jnp.bfloat16),
-        in_specs=in_vmem(3),
+        in_specs=in_vmem(2 + len(arrived)),
         out_specs=in_vmem(1)[0],
         scratch_shapes=[
             pltpu.VMEM((band * (parts * segments + 8), 2 * channels), jnp.float32),
             pltpu.VMEM((band * (channels + 8), 2 * channels), jnp.float32),
         ],
         compiler_params=pltpu.CompilerParams(vmem_limit_bytes=40 * 2**20),
-    )(index, arrived, table)
+    )(index, table, *arrived)
 
     scaling = 1.0 / math.sqrt(frequencies * segments)
     received = lax.all_to_all(message, "seg", split_axis=0, concat_axis=0, tiled=True)
@@ -226,4 +251,4 @@
 def solution(mesh):
     in_specs = (P(None, ("blk", "seg"), None, None), P(), P())
     out_specs = P(None, "blk", "seg", None, None)
-    return jax.shard_map(local, mesh=mesh, in_specs=in_specs, out_specs=out_specs, check_vma=False)
+    return jax.shard_map(stacks, mesh=mesh, in_specs=in_specs, out_specs=out_specs, check_vma=False)

time: 161 us -> 162 us (level)
  waiting for transfers between devices: 71.7 us -> 45.3 us
  starting transfers between devices: 27.1 us -> 48.8 us
  blocking collectives: 31.2 us -> 33.3 us
  local copies, waits for them, and re-layouts: 6.91 us -> 8.94 us
    all_to_all x3, waiting for transfers between devices: 71.7 us -> 22.9 us  [the longest x2 13.8 us: stacks(): lax.all_to_all(bands, 'seg', split_axis=0, concat_axis=0, tiled=True)]
    ppermute x0 -> x14, starting transfers between devices: none -> 35.5 us  [stacks(): pieces[turn] = lax.ppermute(packed[turn], 'blk', turned[turn])]
    ppermute x0 -> x14, waiting for transfers between devices: none -> 22.4 us  [stacks(): pieces[turn] = lax.ppermute(packed[turn], 'blk', turned[turn])]
    all_to_all x3, starting transfers between devices: 27.1 us -> 13.4 us  [the longest x2 9.87 us: stacks(): lax.all_to_all(bands, 'seg', split_axis=0, concat_axis=0, tiled=True)]
    all_to_all x1, blocking collectives: 31.2 us -> 33.3 us  [stacks(): lax.all_to_all(message, 'seg', split_axis=0, concat_axis=0, tiled=True)]
    unnamed x4 -> x12, local copies, waits for them, and re-layouts: 0.01 us -> 2.04 us
    reshape x3 -> x5, local copies, waits for them, and re-layouts: 5.81 us -> 4.66 us  [the longest x4 4.53 us: stacks(): spectra[first:first + size].reshape(size, holders, parts, seg_count, band)]
    pallas_call x2 -> x3, Pallas kernels: 15.5 us -> 16.2 us  [the longest x1 13.2 us: stacks(): pl.pallas_call(functools.partial(pair_kernel, 8, 16), out_shape=jax.Shape...]
  transfers between devices with their start and end apart: 3 -> 17, of which waited for: 3 -> 6; matrix products, arithmetic and copies ran while one was open for 3% -> 5% of each run, Pallas kernels for 0% -> 2%
where the time goes in v3:
time: 162 us; the launch traced here: 161 us
  starting transfers between devices  48.8 us (30%)
  waiting for transfers between devices  45.3 us (28%)
  blocking collectives  33.3 us (21%)
  Pallas kernels  16.2 us (10%)
  local copies, waits for them, and re-layouts  8.94 us (6%)
  other arithmetic  6.1 us (4%)
  between operations  2.76 us (2%)
    ppermute x14, starting transfers between devices, stacks(): pieces[turn] = lax.ppermute(packed[turn], 'blk', turned[turn])  35.5 us
    all_to_all x1, blocking collectives, stacks(): lax.all_to_all(message, 'seg', split_axis=0, concat_axis=0, tiled=True)  33.3 us
    ppermute x14, waiting for transfers between devices, stacks(): pieces[turn] = lax.ppermute(packed[turn], 'blk', turned[turn])  22.4 us
    all_to_all x2, waiting for transfers between devices, stacks(): lax.all_to_all(bands, 'seg', split_axis=0, concat_axis=0, tiled=True)  13.8 us
    pallas_call x1, Pallas kernels, stacks(): pl.pallas_call(functools.partial(pair_kernel, 8, 16), out_shape=jax.Shape...  13.2 us
    all_to_all x2, starting transfers between devices, stacks(): lax.all_to_all(bands, 'seg', split_axis=0, concat_axis=0, tiled=True)  9.87 us
    all_to_all x1, waiting for transfers between devices, stacks(): lax.all_to_all(everyone, 'blk', split_axis=0, concat_axis=0, tiled=True)  9.16 us
    reshape x4, local copies, waits for them, and re-layouts, stacks(): spectra[first:first + size].reshape(size, holders, parts, seg_count, band)  4.53 us
  transfers between devices with their start and end apart: 17, of which 6 were waited for; matrix products, arithmetic and copies ran while one was open for 5% of the time, Pallas kernels for 2%

profile of v3, /device:TPU:0, one launch (start us, length us, event | category | flops | bytes accessed | tf_op | source)
XLA Modules:
  0.0 161.4 jit_solution(12807828180683818869)
XLA Ops:
  0.0 1.1 slice-done
  1.6 1.4 copy.25
  3.0 6.2 %all-to-all-start = ((bf16[16,6,2,8,256]{4,3,2,1,0:T(8,128)(2,1)}), bf16[16,6,2,8,256]{4,3,2,1,0:T(8,128)(2,1)S(1)}, u32[]{:S(2)}, u32[]{:S(2)}) async-start(bf16[16,6,2,8,256]{4,3,2,1,0:T(8,128)(2,1)} %bitcast.22), calls=%async_computation | async-start | bytes 1572864 | tf_op jit(solution)/shard_map/all_to_all | solution.py:176
  9.4 0.9 reshape.203
  10.3 1.8 %copy.24 = bf16[10,8,2,16,256]{4,1,2,0,3:T(8,128)(2,1)} copy(bf16[10,8,2,16,256]{4,3,2,1,0:T(8,128)(2,1)S(1)} %reshape.203) | data formatting | bytes 2621440 | tf_op jit(solution)/shard_map/reshape | solution.py:174
  12.5 10.3 %all-to-all-done.rows_ref = bf16[16,6,2,8,256]{4,3,2,1,0:T(8,128)(2,1)S(1)} async-done(((bf16[16,6,2,8,256]{4,3,2,1,0:T(8,128)(2,1)}), bf16[16,6,2,8,256]{4,3,2,1,0:T(8,128)(2,1)S(1)}, u32[]{:S(2)}, u32[]{:S(2)}) %all-to-all-start) | async-done | bytes 786464 | tf_op jit(solution)/shard_map/all_to_all | solution.py:176
  22.8 3.7 %all-to-all-start.1 = ((bf16[16,10,2,8,256]{4,3,2,1,0:T(8,128)(2,1)}), bf16[16,10,2,8,256]{4,3,2,1,0:T(8,128)(2,1)S(1)}, u32[]{:S(2)}, u32[]{:S(2)}) async-start(bf16[16,10,2,8,256]{4,3,2,1,0:T(8,128)(2,1)} %bitcast.25), calls=%async_computation.1 | async-start | bytes 2621440 | tf_op jit(solution)/shard_map/all_to_all | solution.py:176
  29.6 1.4 shard_map.37
  32.4 1.5 collective-permute-start
  34.6 2.8 %collective-permute-start.1 = (bf16[6,2,24,256]{3,2,1,0:T(8,128)(2,1)}, bf16[6,2,24,256]{3,2,1,0:T(8,128)(2,1)S(1)}, u32[]{:S(2)}, u32[]{:S(2)}) collective-permute-start(bf16[6,2,24,256]{3,2,1,0:T(8,128)(2,1)} %get-tuple-element.23), channel_id=1, source_target_pairs={{0,32},{16,48},{32,0},{48,16},{64,96},{80,112},{96,64},{112,80},{1... | collective-permute-start | bytes 442376 | tf_op jit(solution)/shard_map/ppermute | solution.py:218
  37.4 1.4 collective-permute-start.2
  38.8 3.6 %collective-permute-start.3 = (bf16[6,2,24,256]{3,2,1,0:T(8,128)(2,1)}, bf16[6,2,24,256]{3,2,1,0:T(8,128)(2,1)S(1)}, u32[]{:S(2)}, u32[]{:S(2)}) collective-permute-start(bf16[6,2,24,256]{3,2,1,0:T(8,128)(2,1)} %get-tuple-element.25), channel_id=1, source_target_pairs={{0,64},{16,80},{32,96},{48,112},{64,0},{80,16},{96,32},{112,48},{1... | collective-permute-start | bytes 442376 | tf_op jit(solution)/shard_map/ppermute | solution.py:218
  42.4 3.5 %all-to-all-done.1.rows_ref = bf16[16,10,2,8,256]{4,3,2,1,0:T(8,128)(2,1)S(1)} async-done(((bf16[16,10,2,8,256]{4,3,2,1,0:T(8,128)(2,1)}), bf16[16,10,2,8,256]{4,3,2,1,0:T(8,128)(2,1)S(1)}, u32[]{:S(2)}, u32[]{:S(2)}) %all-to-all-start.1) | async-done | bytes 1310752 | tf_op jit(solution)/shard_map/all_to_all | solution.py:176
  45.9 1.6 shard_map.38
  48.1 1.5 collective-permute-start.7
  49.6 2.7 %collective-permute-start.8 = (bf16[10,2,24,256]{3,2,1,0:T(8,128)(2,1)}, bf16[10,2,24,256]{3,2,1,0:T(8,128)(2,1)S(1)}, u32[]{:S(2)}, u32[]{:S(2)}) collective-permute-start(bf16[10,2,24,256]{3,2,1,0:T(8,128)(2,1)} %get-tuple-element.31), channel_id=1, source_target_pairs={{0,32},{16,48},{32,0},{48,16},{64,96},{80,112},{96,64},{112,80},{1... | collective-permute-start | bytes 737288 | tf_op jit(solution)/shard_map/ppermute | solution.py:218
  52.4 2.9 %collective-permute-start.4 = (bf16[6,2,24,256]{3,2,1,0:T(8,128)(2,1)}, bf16[6,2,24,256]{3,2,1,0:T(8,128)(2,1)S(1)}, u32[]{:S(2)}, u32[]{:S(2)}) collective-permute-start(bf16[6,2,24,256]{3,2,1,0:T(8,128)(2,1)} %copy-done.2), channel_id=1, source_target_pairs={{0,80},{16,96},{32,112},{48,64},{64,16},{80,32},{96,48},{112,0},{1... | collective-permute-start | bytes 442376 | tf_op jit(solution)/shard_map/ppermute | solution.py:218
  55.3 2.4 %collective-permute-start.5 = (bf16[6,2,24,256]{3,2,1,0:T(8,128)(2,1)}, bf16[6,2,24,256]{3,2,1,0:T(8,128)(2,1)S(1)}, u32[]{:S(2)}, u32[]{:S(2)}) collective-permute-start(bf16[6,2,24,256]{3,2,1,0:T(8,128)(2,1)} %copy-done.1), channel_id=1, source_target_pairs={{0,96},{16,112},{32,64},{48,80},{64,32},{80,48},{96,0},{112,16},{1... | collective-permute-start | bytes 442376 | tf_op jit(solution)/shard_map/ppermute | solution.py:218
  57.7 3.6 %collective-permute-start.6 = (bf16[6,2,24,256]{3,2,1,0:T(8,128)(2,1)S(1)}, bf16[6,2,24,256]{3,2,1,0:T(8,128)(2,1)S(1)}, u32[]{:S(2)}, u32[]{:S(2)}) collective-permute-start(bf16[6,2,24,256]{3,2,1,0:T(8,128)(2,1)S(1)} %get-tuple-element.28), channel_id=1, source_target_pairs={{0,112},{16,64},{32,80},{48,96},{64,48},{80,0},{96,16},{112,32},{1... | collective-permute-start | bytes 442376 | tf_op jit(solution)/shard_map/ppermute | solution.py:218
  61.5 7.8 %collective-permute-done.4.refs_5_ = bf16[6,2,24,256]{3,2,1,0:T(8,128)(2,1)S(1)} collective-permute-done((bf16[6,2,24,256]{3,2,1,0:T(8,128)(2,1)}, bf16[6,2,24,256]{3,2,1,0:T(8,128)(2,1)S(1)}, u32[]{:S(2)}, u32[]{:S(2)}) %collective-permute-start.4) | collective-permute-done | bytes 147488 | tf_op jit(solution)/shard_map/ppermute | solution.py:218
  69.3 3.9 %collective-permute-start.9 = (bf16[10,2,24,256]{3,2,1,0:T(8,128)(2,1)}, bf16[10,2,24,256]{3,2,1,0:T(8,128)(2,1)S(1)}, u32[]{:S(2)}, u32[]{:S(2)}) collective-permute-start(bf16[10,2,24,256]{3,2,1,0:T(8,128)(2,1)} %copy-done), channel_id=1, source_target_pairs={{0,48},{16,0},{32,16},{48,32},{64,112},{80,64},{96,80},{112,96},{1... | collective-permute-start | bytes 737288 | tf_op jit(solution)/shard_map/ppermute | solution.py:218
  73.9 1.2 collective-permute-start.11
  75.1 3.0 %collective-permute-start.12 = (bf16[10,2,24,256]{3,2,1,0:T(8,128)(2,1)S(1)}, bf16[10,2,24,256]{3,2,1,0:T(8,128)(2,1)S(1)}, u32[]{:S(2)}, u32[]{:S(2)}) collective-permute-start(bf16[10,2,24,256]{3,2,1,0:T(8,128)(2,1)S(1)} %get-tuple-element.35), channel_id=1, source_target_pairs={{0,96},{16,112},{32,64},{48,80},{64,32},{80,48},{96,0},{112,16},{1... | collective-permute-start | bytes 737288 | tf_op jit(solution)/shard_map/ppermute | solution.py:218
  78.1 5.0 %collective-permute-start.13 = (bf16[10,2,24,256]{3,2,1,0:T(8,128)(2,1)S(1)}, bf16[10,2,24,256]{3,2,1,0:T(8,128)(2,1)S(1)}, u32[]{:S(2)}, u32[]{:S(2)}) collective-permute-start(bf16[10,2,24,256]{3,2,1,0:T(8,128)(2,1)S(1)} %get-tuple-element.36), channel_id=1, source_target_pairs={{0,112},{16,64},{32,80},{48,96},{64,48},{80,0},{96,16},{112,32},{1... | collective-permute-start | bytes 737288 | tf_op jit(solution)/shard_map/ppermute | solution.py:218
  83.7 14.0 %collective-permute-done.10.refs_12_ = bf16[10,2,24,256]{3,2,1,0:T(8,128)(2,1)S(1)} collective-permute-done((bf16[10,2,24,256]{3,2,1,0:T(8,128)(2,1)S(1)}, bf16[10,2,24,256]{3,2,1,0:T(8,128)(2,1)S(1)}, u32[]{:S(2)}, u32[]{:S(2)}) %collective-permute-start.10) | collective-permute-done | bytes 245792 | tf_op jit(solution)/shard_map/ppermute | solution.py:218
  97.7 13.2 %shard_map.39 = bf16[16,128,4,128]{3,2,1,0:T(4,128)(2,1)S(1)} custom-call(s32[128,1]{1,0:T(8,128)S(1)} %reshape.201.index_ref, bf16[256,256]{1,0:T(8,128)(2,1)S(1)} %pad_maximum_fusion.table_ref, bf16[6,2,24,256]{3,2,1,0:T(8,128)(2,1)S(1)} %get-tuple-element.21.refs_0_, bf16[6,2,24,256]{3,2,1,0:T(8,128)(2,1)S(1)} %collective-permute-done.refs_1_, ...), custom_call_target="tpu_custom_call" | custom-call | tf_op jit(solution)/shard_map/pallas_call | solution.py:222
  110.9 33.3 %all_to_all.20 = bf16[16,128,4,128]{3,2,1,0:T(4,128)(2,1)S(1)} all-to-all(bf16[16,128,4,128]{3,2,1,0:T(4,128)(2,1)S(1)} %shard_map.39), channel_id=1, replica_groups=mesh['blk'=8,'seg'=16] {'seg'}, dimensions={0} | all-to-all | bytes 4194304 | tf_op jit(solution)/shard_map/all_to_all | solution.py:235
  144.2 0.9 convert_reduce_fusion
  145.2 0.9 broadcast_in_dim.124
  146.2 3.5 %all-to-all-start.3 = ((bf16[8,4,64,128]{3,2,1,0:T(8,128)(2,1)}), bf16[8,4,64,128]{3,2,1,0:T(8,128)(2,1)S(1)}, u32[]{:S(2)}, u32[]{:S(2)}) async-start(bf16[8,4,64,128]{3,2,1,0:T(8,128)(2,1)} %broadcast_in_dim.124), calls=%async_computation.3 | async-start | bytes 1048576 | tf_op jit(solution)/shard_map/all_to_all | solution.py:240
  151.5 9.2 %all-to-all-done.3 = bf16[8,4,64,128]{3,2,1,0:T(8,128)(2,1)S(1)} async-done(((bf16[8,4,64,128]{3,2,1,0:T(8,128)(2,1)}), bf16[8,4,64,128]{3,2,1,0:T(8,128)(2,1)S(1)}, u32[]{:S(2)}, u32[]{:S(2)}) %all-to-all-start.3) | async-done | bytes 524320 | tf_op jit(solution)/shard_map/all_to_all | solution.py:240
  160.7 0.7 maximum_bitcast_fusion
  (59 shorter events, 8.0 us)
Async XLA Ops:
  0.0 1.1 slice-start
  1.1 8.1 %copy-start.4 = (s32[1,16]{1,0:T(1,128)S(1)}, s32[1,16]{1,0:T(1,128)}, u32[]{:S(2)}) copy-start(s32[1,16]{1,0:T(1,128)} %param.5) | copy-start | bytes 196
  3.0 6.4 %slice-start.1 = ((bf16[16,8,2,4096]{3,2,1,0:T(2,128)(2,1)}), bf16[10,8,2,4096]{3,2,1,0:T(2,128)(2,1)S(1)}, s32[]{:S(2)}) async-start(bf16[16,8,2,4096]{3,2,1,0:T(2,128)(2,1)} %param.3), calls=%async_computation.5 | async-start | bytes 2621440 | tf_op jit(solution)/shard_map/slice | solution.py:174
  3.0 19.8 %all-to-all-start = ((bf16[16,6,2,8,256]{4,3,2,1,0:T(8,128)(2,1)}), bf16[16,6,2,8,256]{4,3,2,1,0:T(8,128)(2,1)S(1)}, u32[]{:S(2)}, u32[]{:S(2)}) async-start(bf16[16,6,2,8,256]{4,3,2,1,0:T(8,128)(2,1)} %bitcast.22), calls=%async_computation | async-start | bytes 1572864 | tf_op jit(solution)/shard_map/all_to_all | solution.py:176
  9.4 3.1 %copy-start.3 = (s32[16,64]{1,0:T(8,128)S(1)}, s32[16,64]{1,0:T(8,128)}, u32[]{:S(2)}) copy-start(s32[16,64]{1,0:T(8,128)} %param.4) | copy-start | bytes 12292
  10.3 18.1 %copy-start.5 = (s32[1,16]{1,0:T(1,128)S(1)}, s32[1,16]{1,0:T(1,128)}, u32[]{:S(2)}) copy-start(s32[1,16]{1,0:T(1,128)} %param.5) | copy-start | bytes 196
  22.8 23.0 %all-to-all-start.1 = ((bf16[16,10,2,8,256]{4,3,2,1,0:T(8,128)(2,1)}), bf16[16,10,2,8,256]{4,3,2,1,0:T(8,128)(2,1)S(1)}, u32[]{:S(2)}, u32[]{:S(2)}) async-start(bf16[16,10,2,8,256]{4,3,2,1,0:T(8,128)(2,1)} %bitcast.25), calls=%async_computation.1 | async-start | bytes 2621440 | tf_op jit(solution)/shard_map/all_to_all | solution.py:176
  31.1 0.7 copy-start.1
  31.7 0.7 copy-start.2
  32.4 17.2 %collective-permute-start = (bf16[6,2,24,256]{3,2,1,0:T(8,128)(2,1)}, bf16[6,2,24,256]{3,2,1,0:T(8,128)(2,1)S(1)}, u32[]{:S(2)}, u32[]{:S(2)}) collective-permute-start(bf16[6,2,24,256]{3,2,1,0:T(8,128)(2,1)} %get-tuple-element.22), channel_id=1, source_target_pairs={{0,16},{16,32},{32,48},{48,0},{64,80},{80,96},{96,112},{112,64},{1... | collective-permute-start | bytes 442376 | tf_op jit(solution)/shard_map/ppermute | solution.py:218
  34.6 17.8 %collective-permute-start.1 = (bf16[6,2,24,256]{3,2,1,0:T(8,128)(2,1)}, bf16[6,2,24,256]{3,2,1,0:T(8,128)(2,1)S(1)}, u32[]{:S(2)}, u32[]{:S(2)}) collective-permute-start(bf16[6,2,24,256]{3,2,1,0:T(8,128)(2,1)} %get-tuple-element.23), channel_id=1, source_target_pairs={{0,32},{16,48},{32,0},{48,16},{64,96},{80,112},{96,64},{112,80},{1... | collective-permute-start | bytes 442376 | tf_op jit(solution)/shard_map/ppermute | solution.py:218
  37.4 17.9 %collective-permute-start.2 = (bf16[6,2,24,256]{3,2,1,0:T(8,128)(2,1)}, bf16[6,2,24,256]{3,2,1,0:T(8,128)(2,1)S(1)}, u32[]{:S(2)}, u32[]{:S(2)}) collective-permute-start(bf16[6,2,24,256]{3,2,1,0:T(8,128)(2,1)} %get-tuple-element.24), channel_id=1, source_target_pairs={{0,48},{16,0},{32,16},{48,32},{64,112},{80,64},{96,80},{112,96},{1... | collective-permute-start | bytes 442376 | tf_op jit(solution)/shard_map/ppermute | solution.py:218
  38.8 18.9 %collective-permute-start.3 = (bf16[6,2,24,256]{3,2,1,0:T(8,128)(2,1)}, bf16[6,2,24,256]{3,2,1,0:T(8,128)(2,1)S(1)}, u32[]{:S(2)}, u32[]{:S(2)}) collective-permute-start(bf16[6,2,24,256]{3,2,1,0:T(8,128)(2,1)} %get-tuple-element.25), channel_id=1, source_target_pairs={{0,64},{16,80},{32,96},{48,112},{64,0},{80,16},{96,32},{112,48},{1... | collective-permute-start | bytes 442376 | tf_op jit(solution)/shard_map/ppermute | solution.py:218
  47.4 0.7 copy-start
  48.1 27.0 %collective-permute-start.7 = (bf16[10,2,24,256]{3,2,1,0:T(8,128)(2,1)}, bf16[10,2,24,256]{3,2,1,0:T(8,128)(2,1)S(1)}, u32[]{:S(2)}, u32[]{:S(2)}) collective-permute-start(bf16[10,2,24,256]{3,2,1,0:T(8,128)(2,1)} %get-tuple-element.30), channel_id=1, source_target_pairs={{0,16},{16,32},{32,48},{48,0},{64,80},{80,96},{96,112},{112,64},{1... | collective-permute-start | bytes 737288 | tf_op jit(solution)/shard_map/ppermute | solution.py:218
  49.6 28.5 %collective-permute-start.8 = (bf16[10,2,24,256]{3,2,1,0:T(8,128)(2,1)}, bf16[10,2,24,256]{3,2,1,0:T(8,128)(2,1)S(1)}, u32[]{:S(2)}, u32[]{:S(2)}) collective-permute-start(bf16[10,2,24,256]{3,2,1,0:T(8,128)(2,1)} %get-tuple-element.31), channel_id=1, source_target_pairs={{0,32},{16,48},{32,0},{48,16},{64,96},{80,112},{96,64},{112,80},{1... | collective-permute-start | bytes 737288 | tf_op jit(solution)/shard_map/ppermute | solution.py:218
  52.4 17.0 %collective-permute-start.4 = (bf16[6,2,24,256]{3,2,1,0:T(8,128)(2,1)}, bf16[6,2,24,256]{3,2,1,0:T(8,128)(2,1)S(1)}, u32[]{:S(2)}, u32[]{:S(2)}) collective-permute-start(bf16[6,2,24,256]{3,2,1,0:T(8,128)(2,1)} %copy-done.2), channel_id=1, source_target_pairs={{0,80},{16,96},{32,112},{48,64},{64,16},{80,32},{96,48},{112,0},{1... | collective-permute-start | bytes 442376 | tf_op jit(solution)/shard_map/ppermute | solution.py:218
  55.3 18.5 %collective-permute-start.5 = (bf16[6,2,24,256]{3,2,1,0:T(8,128)(2,1)}, bf16[6,2,24,256]{3,2,1,0:T(8,128)(2,1)S(1)}, u32[]{:S(2)}, u32[]{:S(2)}) collective-permute-start(bf16[6,2,24,256]{3,2,1,0:T(8,128)(2,1)} %copy-done.1), channel_id=1, source_target_pairs={{0,96},{16,112},{32,64},{48,80},{64,32},{80,48},{96,0},{112,16},{1... | collective-permute-start | bytes 442376 | tf_op jit(solution)/shard_map/ppermute | solution.py:218
  57.7 16.2 %collective-permute-start.6 = (bf16[6,2,24,256]{3,2,1,0:T(8,128)(2,1)S(1)}, bf16[6,2,24,256]{3,2,1,0:T(8,128)(2,1)S(1)}, u32[]{:S(2)}, u32[]{:S(2)}) collective-permute-start(bf16[6,2,24,256]{3,2,1,0:T(8,128)(2,1)S(1)} %get-tuple-element.28), channel_id=1, source_target_pairs={{0,112},{16,64},{32,80},{48,96},{64,48},{80,0},{96,16},{112,32},{1... | collective-permute-start | bytes 442376 | tf_op jit(solution)/shard_map/ppermute | solution.py:218
  69.3 14.3 %collective-permute-start.9 = (bf16[10,2,24,256]{3,2,1,0:T(8,128)(2,1)}, bf16[10,2,24,256]{3,2,1,0:T(8,128)(2,1)S(1)}, u32[]{:S(2)}, u32[]{:S(2)}) collective-permute-start(bf16[10,2,24,256]{3,2,1,0:T(8,128)(2,1)} %copy-done), channel_id=1, source_target_pairs={{0,48},{16,0},{32,16},{48,32},{64,112},{80,64},{96,80},{112,96},{1... | collective-permute-start | bytes 737288 | tf_op jit(solution)/shard_map/ppermute | solution.py:218
  73.8 24.0 %collective-permute-start.10 = (bf16[10,2,24,256]{3,2,1,0:T(8,128)(2,1)S(1)}, bf16[10,2,24,256]{3,2,1,0:T(8,128)(2,1)S(1)}, u32[]{:S(2)}, u32[]{:S(2)}) collective-permute-start(bf16[10,2,24,256]{3,2,1,0:T(8,128)(2,1)S(1)} %get-tuple-element.33), channel_id=1, source_target_pairs={{0,64},{16,80},{32,96},{48,112},{64,0},{80,16},{96,32},{112,48},{1... | collective-permute-start | bytes 737288 | tf_op jit(solution)/shard_map/ppermute | solution.py:218
  73.9 23.8 %collective-permute-start.11 = (bf16[10,2,24,256]{3,2,1,0:T(8,128)(2,1)S(1)}, bf16[10,2,24,256]{3,2,1,0:T(8,128)(2,1)S(1)}, u32[]{:S(2)}, u32[]{:S(2)}) collective-permute-start(bf16[10,2,24,256]{3,2,1,0:T(8,128)(2,1)S(1)} %get-tuple-element.34), channel_id=1, source_target_pairs={{0,80},{16,96},{32,112},{48,64},{64,16},{80,32},{96,48},{112,0},{1... | collective-permute-start | bytes 737288 | tf_op jit(solution)/shard_map/ppermute | solution.py:218
  75.1 22.6 %collective-permute-start.12 = (bf16[10,2,24,256]{3,2,1,0:T(8,128)(2,1)S(1)}, bf16[10,2,24,256]{3,2,1,0:T(8,128)(2,1)S(1)}, u32[]{:S(2)}, u32[]{:S(2)}) collective-permute-start(bf16[10,2,24,256]{3,2,1,0:T(8,128)(2,1)S(1)} %get-tuple-element.35), channel_id=1, source_target_pairs={{0,96},{16,112},{32,64},{48,80},{64,32},{80,48},{96,0},{112,16},{1... | collective-permute-start | bytes 737288 | tf_op jit(solution)/shard_map/ppermute | solution.py:218
  78.1 19.6 %collective-permute-start.13 = (bf16[10,2,24,256]{3,2,1,0:T(8,128)(2,1)S(1)}, bf16[10,2,24,256]{3,2,1,0:T(8,128)(2,1)S(1)}, u32[]{:S(2)}, u32[]{:S(2)}) collective-permute-start(bf16[10,2,24,256]{3,2,1,0:T(8,128)(2,1)S(1)} %get-tuple-element.36), channel_id=1, source_target_pairs={{0,112},{16,64},{32,80},{48,96},{64,48},{80,0},{96,16},{112,32},{1... | collective-permute-start | bytes 737288 | tf_op jit(solution)/shard_map/ppermute | solution.py:218
  146.2 14.5 %all-to-all-start.3 = ((bf16[8,4,64,128]{3,2,1,0:T(8,128)(2,1)}), bf16[8,4,64,128]{3,2,1,0:T(8,128)(2,1)S(1)}, u32[]{:S(2)}, u32[]{:S(2)}) async-start(bf16[8,4,64,128]{3,2,1,0:T(8,128)(2,1)} %broadcast_in_dim.124), calls=%async_computation.3 | async-start | bytes 1048576 | tf_op jit(solution)/shard_map/all_to_all | solution.py:240
